TPU v7x, 32 devices: a whole 2x2x4 slice. The times are simulated.
32 devices in a mesh: cache: 2 (over y), tp: 8 (over z, core), cand: 2 (over x).
Axes of the slice: x: 2, y: 2, z: 4, core: 2. Of those that a mesh axis runs over, the one named last changes fastest.
Arguments:
- prompt_inputs: bfloat16 [1536, 8192], P(('cache', 'cand')), may hold values from -6 to 6
- cand_inputs: bfloat16 [4096, 8192], P(('cache', 'cand'), 'tp'), may hold values from -6 to 6
- norm_gain: float32 [8192], replicated, may hold values from 0.1 to 1.9
- w_query: bfloat16 [8192, 8192], P('cache', 'tp'), may hold values from -0.0625 to 0.0625
- w_key: bfloat16 [8192, 1024], P('cache', 'tp'), may hold values from -0.0625 to 0.0625
- w_value: bfloat16 [8192, 1024], P('cache', 'tp'), may hold values from -0.0625 to 0.0625
- q_bias: float32 [8192], P('tp'), may hold values from -180 to 180
- k_bias: float32 [1024], P('tp'), may hold values from -3 to 8
- v_bias: float32 [1024], P('tp'), may hold values from -4 to 4
- cand_lengths: int32 [16], replicated, may hold values from 32 to 256, as said below
- prefix_ends: int32 [16], replicated, may hold values from 384 to 1536, as said below
Outputs:
- attn_out: bfloat16 [4096, 8192], P(('cache', 'cand'), 'tp')
Inputs may be any that keep to these rules, and one draw needn't show every extreme that they name: `cand_lengths`: at least one candidate has 256 tokens. `prefix_ends`: at least one candidate follows the whole prompt.
All inputs are finite; a program needn't handle non-finite values.
Results may differ from a plain program's by a relative error of at most 0.0075.
The roundings to bfloat16 on the way count: a program that leaves them out, or rounds other values in their place, can miss the bound.
Values may be sent and summed in bfloat16 or wider, within the bound.
A program may use at most 192 MiB of HBM per device.

v0:
```python
import functools
import math

import jax
import jax.numpy as jnp
from jax import lax
from jax.experimental import pallas as pl
from jax.experimental.pallas import tpu as pltpu
from jax.sharding import PartitionSpec as P

D = 8192
HEADS = 64
KV_HEADS = 8
HEAD = 128
CANDS = 16
CLEN = 256


ROPE_THETA = 1000000.0
EPSILON = 1e-06


def rotate(tensor, positions):
    half_size = tensor.shape[-1] // 2
    inverse_freq = jnp.power(
        ROPE_THETA, -jnp.arange(half_size, dtype=jnp.float32) * 2.0 / tensor.shape[-1]
    )
    angles = positions.astype(jnp.float32)[:, None] * inverse_freq[None, :]
    cosine = jnp.cos(angles)[:, None, :]
    sine_part = jnp.sin(angles)[:, None, :]
    first_half = tensor[..., :half_size]
    second = tensor[..., half_size:]
    return jnp.concatenate(
        [first_half * cosine - second * sine_part, second * cosine + first_half * sine_part],
        axis=-1,
    )


def row_lookup(row_ids, table):
    chosen = (row_ids // CLEN)[:, None] == jnp.arange(CANDS, dtype=jnp.int32)[None, :]
    return jnp.sum(jnp.where(chosen, table[None, :], 0), axis=1)


def attend_kernel(
    prefix_ref, length_ref, offset_ref, q_ref, kvp_ref, kvc_ref, out_ref, *, heads, chunk, scale
):
    cand = pl.program_id(0)
    prefix = prefix_ref[cand]
    length = length_ref[cand]
    offset = offset_ref[cand]
    rows = q_ref.shape[0]
    contract = (((1,), (1,)), ((), ()))

    def scores_of(head, key_rows):
        return (
            lax.dot_general(
                q_ref[:, head * HEAD : (head + 1) * HEAD],
                key_rows,
                contract,
                preferred_element_type=jnp.float32,
            )
            * scale
        )

    def weighted(probabilities, value_rows):
        return jnp.dot(
            probabilities.astype(jnp.bfloat16), value_rows, preferred_element_type=jnp.float32
        )

    own_shape = (rows, kvc_ref.shape[0])
    causal = lax.broadcasted_iota(jnp.int32, own_shape, 1) <= offset + lax.broadcasted_iota(
        jnp.int32, own_shape, 0
    )
    state = []
    for head in range(heads):
        scores = jnp.where(causal, scores_of(head, kvc_ref[:, :HEAD]), -1e30)
        maxima = jnp.max(scores, axis=1, keepdims=True)
        probabilities = jnp.exp2(scores - maxima)
        totals = jnp.sum(probabilities, axis=1, keepdims=True)
        state += [maxima, totals, weighted(probabilities, kvc_ref[:, HEAD:])]

    def advance(turn, running):
        first = pl.multiple_of(turn * chunk, chunk)
        key_rows = kvp_ref[pl.ds(first, chunk), :HEAD]
        value_rows = kvp_ref[pl.ds(first, chunk), HEAD:]
        seen = first + lax.broadcasted_iota(jnp.int32, (rows, chunk), 1) < prefix
        following = []
        for head in range(heads):
            maxima, totals, accumulated = running[3 * head : 3 * head + 3]
            scores = jnp.where(seen, scores_of(head, key_rows), -1e30)
            new_maxima = jnp.maximum(maxima, jnp.max(scores, axis=1, keepdims=True))
            probabilities = jnp.exp2(scores - new_maxima)
            rescale = jnp.exp2(maxima - new_maxima)
            totals = totals * rescale + jnp.sum(probabilities, axis=1, keepdims=True)
            accumulated = accumulated * rescale + weighted(probabilities, value_rows)
            following += [new_maxima, totals, accumulated]
        return tuple(following)

    state = lax.fori_loop(0, (prefix + chunk - 1) // chunk, advance, tuple(state))
    valid = offset + lax.broadcasted_iota(jnp.int32, (rows, HEAD), 0) < length
    for head in range(heads):
        result = state[3 * head + 2] / state[3 * head + 1]
        out_ref[:, head * HEAD : (head + 1) * HEAD] = jnp.where(valid, result, 0.0).astype(
            jnp.bfloat16
        )


def attend(prefixes, lengths, offsets, queries, kv_prompt, kv_cand, kv_local, groups):
    tiles = prefixes.shape[0]
    rows = queries.shape[0] // tiles
    prompt = kv_prompt.shape[0]
    chunk = next(size for size in (512, 256, 128, prompt) if prompt % size == 0)
    heads = 2 if groups % 2 == 0 else 1
    turns = groups // heads
    return pl.pallas_call(
        functools.partial(
            attend_kernel, heads=heads, chunk=chunk, scale=HEAD ** (-0.5) * math.log2(math.e)
        ),
        grid_spec=pltpu.PrefetchScalarGridSpec(
            num_scalar_prefetch=3,
            grid=(tiles, kv_local, turns),
            in_specs=[
                pl.BlockSpec((rows, heads * HEAD), lambda c, k, t, *_: (c, k * turns + t)),
                pl.BlockSpec((prompt, 2 * HEAD), lambda c, k, t, *_: (0, k)),
                pl.BlockSpec((CLEN, 2 * HEAD), lambda c, k, t, *_: (c, k)),
            ],
            out_specs=pl.BlockSpec((rows, heads * HEAD), lambda c, k, t, *_: (c, k * turns + t)),
        ),
        out_shape=jax.ShapeDtypeStruct(queries.shape, jnp.bfloat16),
        cost_estimate=pl.CostEstimate(
            flops=4 * queries.size * (prompt + CLEN),
            bytes_accessed=4 * queries.size,
            transcendentals=queries.size // HEAD * (prompt + CLEN),
        ),
        compiler_params=pltpu.CompilerParams(vmem_limit_bytes=60 * 1024 * 1024),
    )(prefixes, lengths, offsets, queries, kv_prompt, kv_cand)


def query_product(normed, w_query):
    caches = lax.axis_size("cache")
    cands = lax.axis_size("cand")
    depth = w_query.shape[0]
    if caches != 2 or cands != 2 or depth % 4 != 0:
        return jnp.dot(
            normed,
            lax.all_gather(w_query, "cache", axis=0, tiled=True),
            preferred_element_type=jnp.float32,
        )
    mine = lax.axis_index("cache")
    side = lax.axis_index("cand")
    part = depth // 4
    swap = [(0, 1), (1, 0)]
    direct = [
        lax.ppermute(
            lax.dynamic_slice_in_dim(w_query, (2 * side + turn) * part, part), "cache", swap
        )
        for turn in range(2)
    ]
    relayed = [lax.ppermute(piece, "cand", swap) for piece in direct]

    def product(first, weights):
        columns = lax.dynamic_slice_in_dim(normed, first, weights.shape[0], 1)
        return jnp.dot(columns, weights, preferred_element_type=jnp.float32)

    total = product(mine * depth, w_query)
    other = (1 - mine) * depth
    for turn in range(2):
        total = total + product(other + (2 * side + turn) * part, direct[turn])
    for turn in range(2):
        total = total + product(other + (2 * (1 - side) + turn) * part, relayed[turn])
    return total


def per_device(
    prompt_inputs,
    cand_inputs,
    norm_gain,
    w_query,
    w_key,
    w_value,
    q_bias,
    k_bias,
    v_bias,
    cand_lengths,
    prefix_ends,
):
    prompt_dev = prompt_inputs.shape[0]
    cand_dev = cand_inputs.shape[0]
    head_size = HEAD
    kv_local = w_key.shape[1] // head_size
    groups = HEADS // KV_HEADS
    kv_width = kv_local * head_size
    joined = lax.axis_index("cache") * lax.axis_size("cand") + lax.axis_index("cand")
    widened_p = prompt_inputs.astype(jnp.float32)
    normed_p = (
        widened_p
        * lax.rsqrt(jnp.mean(widened_p * widened_p, axis=-1, keepdims=True) + EPSILON)
        * norm_gain
    ).astype(jnp.bfloat16)
    widened_c = cand_inputs.astype(jnp.float32)
    squares = lax.psum(jnp.sum(widened_c * widened_c, axis=-1), "tp")
    part_width = cand_inputs.shape[1]
    gain_part = lax.dynamic_slice_in_dim(norm_gain, lax.axis_index("tp") * part_width, part_width)
    normed_part = (widened_c * lax.rsqrt(squares / D + EPSILON)[:, None] * gain_part).astype(
        jnp.bfloat16
    )
    normed_c = lax.all_gather(normed_part, "tp", axis=1, tiled=True)
    row_ids = joined * cand_dev + jnp.arange(cand_dev, dtype=jnp.int32)
    prefix_row = row_lookup(row_ids, prefix_ends)
    cand_pos = prefix_row + row_ids % CLEN
    prompt_pos = joined * prompt_dev + jnp.arange(prompt_dev, dtype=jnp.int32)
    key_value = jnp.concatenate([w_key, w_value], axis=1)
    if lax.axis_size("cache") == 2:
        other_half = lax.ppermute(key_value, "cache", [(0, 1), (1, 0)])
        key_value = jnp.where(
            lax.axis_index("cache") == 0,
            jnp.concatenate([key_value, other_half], axis=0),
            jnp.concatenate([other_half, key_value], axis=0),
        )
    else:
        key_value = lax.all_gather(key_value, "cache", axis=0, tiled=True)
    kv_prompt = jnp.dot(normed_p, key_value, preferred_element_type=jnp.float32)

    def keys_values(product, positions):
        rows = product.shape[0]
        keys = rotate(
            (product[:, :kv_width] + k_bias).reshape(rows, kv_local, head_size), positions
        ).astype(jnp.bfloat16)
        values = (product[:, kv_width:] + v_bias).astype(jnp.bfloat16)
        values = values.reshape(rows, kv_local, head_size)
        return jnp.concatenate([keys, values], axis=2).reshape(rows, 2 * kv_width)

    kv_p = lax.all_gather(
        keys_values(kv_prompt, prompt_pos), ("cache", "cand"), axis=0, tiled=True
    )
    q_cand = query_product(normed_c, w_query)
    kv_c = keys_values(jnp.dot(normed_c, key_value, preferred_element_type=jnp.float32), cand_pos)
    queries = rotate(
        (q_cand + q_bias).reshape(cand_dev, kv_local * groups, head_size), cand_pos
    ).astype(jnp.bfloat16)
    tile_rows = min(cand_dev, CLEN)
    tile_first = joined * cand_dev + tile_rows * jnp.arange(cand_dev // tile_rows, dtype=jnp.int32)
    prefixes = row_lookup(tile_first, prefix_ends)
    lengths = row_lookup(tile_first, cand_lengths)
    offsets = tile_first % CLEN
    if cand_dev < CLEN:
        kv_c = lax.all_gather(kv_c, ("cache", "cand"), axis=0, tiled=True)
        kv_c = lax.dynamic_slice_in_dim(kv_c, joined * cand_dev // CLEN * CLEN, CLEN)
    return attend(
        prefixes,
        lengths,
        offsets,
        queries.reshape(cand_dev, kv_local * groups * head_size),
        kv_p,
        kv_c,
        kv_local,
        groups,
    )


def solution(mesh):
    placed = (
        P(("cache", "cand"), None),
        P(("cache", "cand"), "tp"),
        P(),
        P("cache", "tp"),
        P("cache", "tp"),
        P("cache", "tp"),
        P("tp"),
        P("tp"),
        P("tp"),
        P(),
        P(),
    )
    return jax.shard_map(
        per_device,
        mesh=mesh,
        in_specs=placed,
        out_specs=P(("cache", "cand"), "tp"),
        check_vma=False,
    )
```

profile of v0, /device:TPU:0, one launch (start us, length us, event | category | flops | bytes accessed | tf_op | source)
XLA Modules:
  0.0 354.3 jit_solution(3920293849003582764)
XLA Ops:
  6.5 2.1 fusion.9
  8.6 18.1 %psum.7 = f32[1024]{0:T(1024)S(1)} all-reduce(f32[1024]{0:T(1024)S(1)} %fusion.9), channel_id=1, replica_groups=mesh['cache'=2,'tp'=8,'cand'=2] {'tp'}, use_global_device_ids=true, to_apply=%region_3.4 | all-reduce | flops 1024 | bytes 8192 | tf_op jit(solution)/shard_map/psum | solution.py:201
  27.4 3.5 fusion.11
  31.0 4.1 %constant_dynamic-slice_fusion = (bf16[1024,1024]{1,0:T(8,128)(2,1)S(1)}, bf16[1024,1024]{1,0:T(8,128)(2,1)}) fusion(bf16[4096,1024]{1,0:T(8,128)(2,1)} %param.14, s32[]{:T(128)S(6)} %select_n.88, s32[]{:T(128)S(6)} %select_n.86), kind=kLoop, calls=%fused_computation.92 | loop fusion | bytes 8388616 | tf_op jit(solution)/shard_map/dynamic_slice | solution.py:155
  35.1 1.5 collective-permute-start.1
  42.3 4.2 %fusion = f32[384]{0:T(512)S(1)} fusion(bf16[384,8192]{1,0:T(8,128)(2,1)} %param.11), kind=kLoop, calls=%fused_computation.2 | loop fusion | flops 9436800 | bytes 6292992 | tf_op jit(solution)/shard_map/reduce_sum | solution.py:197
  46.5 1.9 multiply_cosine_fusion.1
  48.5 80.2 %collective-permute-done = bf16[1024,1024]{1,0:T(8,128)(2,1)} collective-permute-done((bf16[1024,1024]{1,0:T(8,128)(2,1)}, bf16[1024,1024]{1,0:T(8,128)(2,1)}, u32[]{:S(2)}, u32[]{:S(2)}) %collective-permute-start) | collective-permute-done | bytes 2097184 | tf_op jit(solution)/shard_map/ppermute | solution.py:154
  130.7 39.0 %collective-permute-done.4 = bf16[4096,256]{1,0:T(8,128)(2,1)} collective-permute-done((bf16[4096,256]{1,0:T(8,128)(2,1)}, bf16[4096,256]{1,0:T(8,128)(2,1)}, u32[]{:S(2)}, u32[]{:S(2)}) %collective-permute-start.4) | collective-permute-done | bytes 2097184 | tf_op jit(solution)/shard_map/ppermute | solution.py:214
  169.6 8.4 %fusion.5 = f32[384,256]{1,0:T(8,128)S(1)} fusion(bf16[384,8192]{1,0:T(8,128)(2,1)} %param.11, f32[8192]{0:T(1024)S(1)} %copy-done.7, f32[384]{0:T(512)S(1)} %add_rsqrt_fusion.1, bf16[4096,256]{1,0:T(8,128)(2,1)} %collective-permute-done.4, bf16[4096,256]{1,0:T(8,128)(2,1)} %constant_dynamic-update-slice_fusion, pred[]{:T(512)S(6)} %eq.23), kind=kOutput, calls=%fused_computation.7 | convolution fusion | flops 1642070016 | bytes 10913281 | tf_op jit(solution)/shard_map/dot_general | solution.py:222
  179.1 44.3 %all-gather = bf16[1536,1,256]{2,0,1:T(8,128)(2,1)} all-gather(bf16[384,1,256]{2,0,1:T(8,128)(2,1)S(1)} %pad_maximum_fusion.1), channel_id=2, replica_groups=mesh['cache'=2,'tp'=8,'cand'=2] {'cache','cand'}, dimensions={0}, use_global_device_ids=true | all-gather | bytes 983040 | tf_op jit(solution)/shard_map/all_gather | solution.py:233
  223.3 4.7 %fusion.16 = f32[1024,1024]{0,1:T(8,128)S(1)} fusion(bf16[1024,1024]{1,0:T(8,128)(2,1)} %collective-permute-done.1, bf16[1024,8192]{1,0:T(8,128)(2,1)} %all-gather.3.cloned.1.call-done, s32[]{:T(128)S(6)} %select_n.87), kind=kOutput, calls=%fused_computation.25 | convolution fusion | flops 2147483648 | bytes 8388612 | tf_op jit(solution)/shard_map/dot_general | solution.py:163
  228.0 4.7 %fusion.18 = f32[1024,1024]{0,1:T(8,128)S(1)} fusion(bf16[1024,1024]{1,0:T(8,128)(2,1)} %collective-permute-done, bf16[1024,8192]{1,0:T(8,128)(2,1)} %all-gather.3.cloned.1.call-done, s32[]{:T(128)S(6)} %select_n.85), kind=kOutput, calls=%fused_computation.27 | convolution fusion | flops 2147483648 | bytes 8388612 | tf_op jit(solution)/shard_map/dot_general | solution.py:163
  232.8 6.6 %fusion.14 = f32[1024,1024]{0,1:T(8,128)} fusion(bf16[1024,1024]{1,0:T(8,128)(2,1)} %collective-permute-done.2, bf16[1024,8192]{1,0:T(8,128)(2,1)} %all-gather.3.cloned.1.call-done, s32[]{:T(128)S(6)} %select_n.89), kind=kOutput, calls=%fused_computation.23 | convolution fusion | flops 2147483648 | bytes 8388612 | tf_op jit(solution)/shard_map/dot_general | solution.py:163
  239.3 15.1 %fusion.3 = f32[1024,1024]{0,1:T(8,128)} fusion(bf16[4096,1024]{1,0:T(8,128)(2,1)} %param.14, bf16[1024,8192]{1,0:T(8,128)(2,1)} %all-gather.3.cloned.1.call-done, s32[]{:T(128)S(6)} %select_n.84), kind=kOutput, calls=%fused_computation.5 | convolution fusion | flops 8589934592 | bytes 20971524 | tf_op jit(solution)/shard_map/dot_general | solution.py:163
  254.4 8.4 %add_add_fusion = f32[1024,1024]{0,1:T(8,128)S(1)} fusion(f32[1024,1024]{0,1:T(8,128)} %fusion.14, f32[1024,1024]{0,1:T(8,128)S(1)} %fusion.16, f32[1024,1024]{0,1:T(8,128)} %fusion.3, f32[1024,1024]{0,1:T(8,128)S(1)} %fusion.18, f32[1024]{0:T(1024)S(1)} %copy-done.2, bf16[1024,1024]{1,0:T(8,128)(2,1)} %collective-permute-done.3, ...), kind=kOutput, calls=%fused_computation.18 | convolution fusion | flops 2152726528 | bytes 25169924 | tf_op jit(solution)/shard_map/dot_general | solution.py:163
  262.8 1.7 fusion.59
  264.6 3.9 %copy.34 = f32[1024,8,64]{2,1,0:T(8,128)} copy(f32[1024,8,64]{0,2,1:T(8,128)} %get-tuple-element.12) | data formatting | bytes 4194304
  268.4 2.7 copy.35
  271.2 4.3 %subtract_convert_fusion = (bf16[1024,8,64]{2,1,0:T(8,128)(2,1)S(1)}, bf16[1024,8,64]{2,1,0:T(8,128)(2,1)S(1)}) fusion(f32[1024,8,64]{2,1,0:T(8,128)} %copy.35, f32[1024,8,64]{2,1,0:T(8,128)} %copy.34, f32[1024,64]{1,0:T(8,128)S(1)} %get-tuple-element.22, f32[1024,64]{1,0:T(8,128)S(1)} %get-tuple-element.21), kind=kLoop, calls=%fused_computation.17 | loop fusion | flops 4194304 | bytes 6815744 | tf_op jit(solution)/shard_map/convert.4
  276.6 2.0 copy.38
  278.6 12.8 %fusion.26 = f32[1024,256]{1,0:T(8,128)S(1)} fusion(bf16[1024,8192]{1,0:T(8,128)(2,1)} %all-gather.3.cloned.1.call-done, bf16[4096,256]{1,0:T(8,128)(2,1)} %collective-permute-done.4, bf16[4096,256]{1,0:T(8,128)(2,1)} %constant_dynamic-update-slice_fusion, pred[]{:T(512)S(6)} %eq.23), kind=kOutput, calls=%fused_computation.37 | convolution fusion | flops 4313841664 | bytes 22020096 | tf_op jit(solution)/shard_map/dot_general | solution.py:237
  291.4 2.4 fusion.28
  294.9 52.6 %shard_map.109 = bf16[1024,1024]{1,0:T(8,128)(2,1)} custom-call(s32[4]{0:T(128)} %get-tuple-element.6.prefix_ref, s32[4]{0:T(128)} %get-tuple-element.5.length_ref, s32[4]{0:T(128)} %and_select_fusion.offset_ref, bf16[1024,1024]{1,0:T(8,128)(2,1)} %bitcast.24, bf16[1536,256]{1,0:T(8,128)(2,1)} %bitcast.25, bf16[1024,256]{1,0:T(8,128)(2,1)} %maximum_bitcast_fusion.kvc_ref), custom_call_target="tpu_custom_call" | custom-call | flops 7516192768 | bytes 4194304 | tf_op jit(solution)/shard_map/pallas_call | solution.py:115
  (45 shorter events, 11.7 us)
Async XLA Ops:
  6.5 216.8 %all-gather.3.cloned.1.call-start = ((), (), s32[]{:S(2)}) async-start(), calls=%async_computation | async-start | bytes 18874368 | tf_op jit(solution)/shard_map/all_gather | solution.py:207
  30.9 6.2 %copy-start = (bf16[4096,128]{1,0:T(8,128)(2,1)S(1)}, bf16[4096,128]{1,0:T(8,128)(2,1)}, u32[]{:S(2)}) copy-start(bf16[4096,128]{1,0:T(8,128)(2,1)} %param.15) | copy-start | bytes 3145732
  30.9 7.3 %copy-start.1 = (bf16[4096,128]{1,0:T(8,128)(2,1)S(1)}, bf16[4096,128]{1,0:T(8,128)(2,1)}, u32[]{:S(2)}) copy-start(bf16[4096,128]{1,0:T(8,128)(2,1)} %param.16) | copy-start | bytes 3145732
  35.1 6.4 %copy-start.3 = (s32[16]{0:T(128)S(1)}, s32[16]{0:T(128)}, u32[]{:S(2)}) copy-start(s32[16]{0:T(128)} %param.21) | copy-start | bytes 196
  35.1 6.4 %copy-start.6 = (s32[16]{0:T(128)S(1)}, s32[16]{0:T(128)}, u32[]{:S(2)}) copy-start(s32[16]{0:T(128)} %param.20) | copy-start | bytes 196
  35.1 95.0 %collective-permute-start.1 = (bf16[1024,1024]{1,0:T(8,128)(2,1)S(1)}, bf16[1024,1024]{1,0:T(8,128)(2,1)}, u32[]{:S(2)}, u32[]{:S(2)}) collective-permute-start(bf16[1024,1024]{1,0:T(8,128)(2,1)S(1)} %get-tuple-element.9), channel_id=1, source_target_pairs={{0,16},{16,0},{1,17},{17,1},{2,18},{18,2},{3,19},{19,3},{4,20},{20... | collective-permute-start | bytes 6291464 | tf_op jit(solution)/shard_map/ppermute | solution.py:154
  36.6 92.0 %collective-permute-start = (bf16[1024,1024]{1,0:T(8,128)(2,1)}, bf16[1024,1024]{1,0:T(8,128)(2,1)}, u32[]{:S(2)}, u32[]{:S(2)}) collective-permute-start(bf16[1024,1024]{1,0:T(8,128)(2,1)} %get-tuple-element.10), channel_id=1, source_target_pairs={{0,16},{16,0},{1,17},{17,1},{2,18},{18,2},{3,19},{19,3},{4,20},{20... | collective-permute-start | bytes 6291464 | tf_op jit(solution)/shard_map/ppermute | solution.py:154
  39.3 130.3 %copy-start.7 = (f32[8192]{0:T(1024)S(1)}, f32[8192]{0:T(1024)}, u32[]{:S(2)}) copy-start(f32[8192]{0:T(1024)} %param.13) | copy-start | bytes 98308
  39.3 130.3 %collective-permute-start.4 = (bf16[4096,256]{1,0:T(8,128)(2,1)}, bf16[4096,256]{1,0:T(8,128)(2,1)}, u32[]{:S(2)}, u32[]{:S(2)}) collective-permute-start(bf16[4096,256]{1,0:T(8,128)(2,1)} %constant_dynamic-update-slice_fusion), channel_id=1, source_target_pairs={{0,16},{16,0},{1,17},{17,1},{2,18},{18,2},{3,19},{19,3},{4,20},{20... | collective-permute-start | bytes 6291464 | tf_op jit(solution)/shard_map/ppermute | solution.py:214
  48.4 129.6 %copy-start.4 = (f32[128]{0:T(128)S(1)}, f32[128]{0:T(128)}, u32[]{:S(2)}) copy-start(f32[128]{0:T(128)} %param.18) | copy-start | bytes 1540
  48.4 129.6 %copy-start.5 = (f32[128]{0:T(128)S(1)}, f32[128]{0:T(128)}, u32[]{:S(2)}) copy-start(f32[128]{0:T(128)} %param.19) | copy-start | bytes 1540
  128.6 104.1 %collective-permute-start.2 = (bf16[1024,1024]{1,0:T(8,128)(2,1)}, bf16[1024,1024]{1,0:T(8,128)(2,1)}, u32[]{:S(2)}, u32[]{:S(2)}) collective-permute-start(bf16[1024,1024]{1,0:T(8,128)(2,1)} %collective-permute-done), channel_id=1, source_target_pairs={{0,1},{1,0},{2,3},{3,2},{4,5},{5,4},{6,7},{7,6},{8,9},{9,8},{10,11... | collective-permute-start | bytes 6291464 | tf_op jit(solution)/shard_map/ppermute | solution.py:159
  130.1 124.3 %collective-permute-start.3 = (bf16[1024,1024]{1,0:T(8,128)(2,1)}, bf16[1024,1024]{1,0:T(8,128)(2,1)}, u32[]{:S(2)}, u32[]{:S(2)}) collective-permute-start(bf16[1024,1024]{1,0:T(8,128)(2,1)} %collective-permute-done.1), channel_id=1, source_target_pairs={{0,1},{1,0},{2,3},{3,2},{4,5},{5,4},{6,7},{7,6},{8,9},{9,8},{10,11... | collective-permute-start | bytes 6291464 | tf_op jit(solution)/shard_map/ppermute | solution.py:159
  239.3 15.1 %copy-start.2 = (f32[1024]{0:T(1024)S(1)}, f32[1024]{0:T(1024)}, u32[]{:S(2)}) copy-start(f32[1024]{0:T(1024)} %param.17) | copy-start | bytes 12292
Sparse Core Ops, SparseCore 0:
  31.0 149.2 all-gather.2
where the time goes:
time: 352 us; the launch traced here: 354 us
  waiting for transfers between devices  119 us (34%)
  blocking collectives  62.4 us (18%)
  matrix products  60.6 us (17%)
  Pallas kernels  52.6 us (15%)
  other arithmetic  23.1 us (7%)
  local copies, waits for them, and re-layouts  17.4 us (5%)
  between operations  13.6 us (4%)
  starting transfers between devices  5.57 us (2%)
    ppermute x2, waiting for transfers between devices, query_product(): lax.ppermute(lax.dynamic_slice_in_dim(w_query, (2 * side + turn) * part,...  80.2 us
    pallas_call x1, Pallas kernels, attend(): pl.pallas_call(functools.partial(attend_kernel, heads=heads, chunk=chunk,...  52.6 us
    all_gather x1, blocking collectives, per_device(): lax.all_gather(keys_values(kv_prompt, prompt_pos), ('cache', 'cand'), axi...  44.3 us
    dot_general x5, matrix products, product(): return jnp.dot(columns, weights, preferred_element_type=jnp.float32)  39.4 us
    ppermute x1, waiting for transfers between devices, per_device(): other_half = lax.ppermute(key_value, 'cache', [(0, 1), (1, 0)])  39 us
    psum x1, blocking collectives, per_device(): squares = lax.psum(jnp.sum(widened_c * widened_c, axis=-1), 'tp')  18.1 us
    dot_general x1, matrix products, per_device(): jnp.dot(normed_c, key_value, preferred_element_type=jnp.float32)  12.8 us
    unnamed x20, local copies, waits for them, and re-layouts  9.69 us
  transfers between devices with their start and end apart: 6, of which 2 were waited for; matrix products, arithmetic and copies ran while one was open for 15% of the time, Pallas kernels for 0%

commit v1 on v0

--- a/solution.py
+++ b/solution.py
@@ -3,6 +3,7 @@
 
 import jax
 import jax.numpy as jnp
+import numpy as np
 from jax import lax
 from jax.experimental import pallas as pl
 from jax.experimental.pallas import tpu as pltpu
@@ -136,6 +137,478 @@
     )(prefixes, lengths, offsets, queries, kv_prompt, kv_cand)
 
 
+MESH = pl.DeviceIdType.MESH
+
+
+def link_orders(depths, chunks):
+    orders = [[(0, r) for r in range(chunks)]]
+    for depth in range(1, depths):
+        ready = {(d + 1, r): k + 2 for k, (d, r) in enumerate(orders[-1])}
+        ready.update({(0, r): 0 for r in range(chunks)})
+        order = []
+        while ready:
+            slot = len(order)
+            able = [e for e in ready if ready[e] <= slot] or list(ready)
+            pick = min(able, key=lambda e: (e[1], e[0]))
+            del ready[pick]
+            order.append(pick)
+        orders.append(order)
+    return orders
+
+
+def project_kernel(
+    xc_ref, xp_ref, gain_ref, wq_ref, wk_ref, wv_ref, qb_ref, kb_ref, vb_ref, freq_ref, prefix_ref,
+    q_ref, kvc_ref, kvp_ref,
+    acts, wts, prompt, cosines, sines, stats,
+    load_sem, wsend, wrecv, rsend, rrecv, own_sem, fwd_sem, sib_sem, arr_sem, st_send, st_recv, kp_send, kp_recv,
+):
+    y, tp, x = lax.axis_index("cache"), lax.axis_index("tp"), lax.axis_index("cand")
+    tps = lax.axis_size("tp")
+    floors = tps // 2
+    z, core = tp // 2, tp % 2
+    rows, part = xc_ref.shape
+    block = CLEN
+    chunks = rows // block
+    half = wq_ref.shape[0]
+    quarter = half // 2
+    piece_rows = quarter // 2
+    wide = 2 * HEAD
+    columns = wq_ref.shape[1] // wide
+    pieces = 2 + 2 * columns
+    prompt_rows = xp_ref.shape[0]
+    slices = tps
+    joined = y * 2 + x
+
+    up, down, sib = (y, tp + 2, x), (y, tp - 2, x), (y, tp + 1 - 2 * core, x)
+    over, aside, across = (1 - y, tp, x), (y, tp, 1 - x), (1 - y, tp, 1 - x)
+    peers = [(y, (tp + t) % tps, x) for t in range(1, tps)]
+
+    barrier = pltpu.get_barrier_semaphore()
+    for peer in peers + [over, aside, across]:
+        pl.semaphore_signal(barrier, inc=1, device_id=peer, device_id_type=MESH)
+
+    load_x = pltpu.make_async_copy(xc_ref, acts.at[tp], load_sem.at[0])
+    load_p = pltpu.make_async_copy(xp_ref, prompt, load_sem.at[1])
+    own_rows = pl.ds(pl.multiple_of(y * half, half), half)
+    load_w = [
+        pltpu.make_async_copy(wk_ref, wts.at[0, own_rows, :HEAD], load_sem.at[2]),
+        pltpu.make_async_copy(wv_ref, wts.at[0, own_rows, HEAD:], load_sem.at[3]),
+    ] + [
+        pltpu.make_async_copy(
+            wq_ref.at[:, j * wide : (j + 1) * wide], wts.at[1 + j, own_rows, :], load_sem.at[4 + j]
+        )
+        for j in range(columns)
+    ]
+    load_x.start()
+    load_p.start()
+    for copy in load_w:
+        copy.start()
+
+    def piece_place(i, side_y, side_x):
+        base = side_y * half + side_x * quarter
+        if i < 2:
+            where = pl.ds(pl.multiple_of(base, quarter), quarter)
+            return wts.at[0, where, i * HEAD : (i + 1) * HEAD]
+        j, h = divmod(i - 2, 2)
+        where = pl.ds(pl.multiple_of(base + h * piece_rows, piece_rows), piece_rows)
+        return wts.at[1 + j, where, :]
+
+    def direct(i):
+        if i < 2:
+            src = (wk_ref, wv_ref)[i].at[pl.ds(pl.multiple_of(x * quarter, quarter), quarter), :]
+        else:
+            j, h = divmod(i - 2, 2)
+            where = pl.ds(pl.multiple_of(x * quarter + h * piece_rows, piece_rows), piece_rows)
+            src = wq_ref.at[where, j * wide : (j + 1) * wide]
+        return pltpu.make_async_remote_copy(
+            src_ref=src, dst_ref=piece_place(i, y, x), send_sem=wsend.at[i], recv_sem=wrecv.at[i],
+            device_id=over, device_id_type=MESH,
+        )
+
+    def relay(i):
+        place = piece_place(i, 1 - y, x)
+        return pltpu.make_async_remote_copy(
+            src_ref=place, dst_ref=place, send_sem=rsend.at[i], recv_sem=rrecv.at[i],
+            device_id=aside, device_id_type=MESH,
+        )
+
+    def pass_piece(i):
+        if 0 <= i < pieces:
+            direct(i).wait_recv()
+            relay(i).start()
+
+    def send_piece(i):
+        if 0 <= i < pieces:
+            direct(i).start()
+
+    def slab(s, r):
+        return acts.at[s, pl.ds(r * block, block), :]
+
+    def slab_copy(s, r, send, target):
+        return pltpu.make_async_remote_copy(
+            src_ref=slab(s, r), dst_ref=slab(s, r), send_sem=send, recv_sem=arr_sem.at[s, r],
+            device_id=target, device_id_type=MESH,
+        )
+
+    def to_sibling(s, r):
+        return slab_copy(s, r, sib_sem.at[s, r], sib)
+
+    def forward(s, r, target):
+        return slab_copy(s, r, fwd_sem.at[s, r], target)
+
+    def own(r, way):
+        return slab_copy(tp, r, own_sem.at[way, r], (up, down)[way])
+
+    orders = link_orders(floors - 1, chunks)
+    longest = orders[-1]
+
+    def link_event(k):
+        if 0 <= k - 2 < len(longest):
+            distance, r = longest[k - 2]
+
+            @pl.when(z == 0)
+            def _():
+                s = tp + 2 * (distance + 1)
+                forward(s, r, down).wait_recv()
+                to_sibling(s, r).start()
+
+            @pl.when(z == floors - 1)
+            def _():
+                s = tp - 2 * (distance + 1)
+                forward(s, r, up).wait_recv()
+                to_sibling(s, r).start()
+
+        for depth, order in enumerate(orders):
+            if k >= len(order):
+                continue
+            distance, r = order[k]
+
+            def go(way, sign, target):
+                if distance == 0:
+                    own(r, way).start()
+                else:
+                    s = tp + sign * 2 * distance
+                    copy = forward(s, r, target)
+                    copy.wait_recv()
+                    copy.start()
+                    to_sibling(s, r).start()
+
+            pl.when(z == depth)(functools.partial(go, 0, -1, up))
+            pl.when(floors - 1 - z == depth)(functools.partial(go, 1, 1, down))
+
+    load_x.wait()
+    for r in range(chunks):
+        wide_x = acts[tp, pl.ds(r * block, block), :].astype(jnp.float32)
+        squares = wide_x * wide_x
+        lanes = squares[:, :HEAD]
+        for t in range(1, part // HEAD):
+            lanes = lanes + squares[:, t * HEAD : (t + 1) * HEAD]
+        for b in range(block // HEAD):
+            turned = jnp.transpose(lanes[b * HEAD : (b + 1) * HEAD, :])
+            stats[tp, :, pl.ds(r * block + b * HEAD, HEAD)] = jnp.sum(turned, axis=0, keepdims=True)
+
+    pl.semaphore_wait(barrier, tps + 2)
+
+    def stat_copy(t):
+        return pltpu.make_async_remote_copy(
+            src_ref=stats.at[tp], dst_ref=stats.at[tp], send_sem=st_send.at[t], recv_sem=st_recv.at[tp],
+            device_id=peers[t], device_id_type=MESH,
+        )
+
+    def stat_arrival(t):
+        s = (tp + 1 + t) % tps
+        return pltpu.make_async_remote_copy(
+            src_ref=stats.at[s], dst_ref=stats.at[s], send_sem=st_send.at[t], recv_sem=st_recv.at[s],
+            device_id=peers[t], device_id_type=MESH,
+        )
+
+    for t in range(tps - 1):
+        stat_copy(t).start()
+    for i in range(4):
+        send_piece(i)
+    for t in range(tps - 1):
+        stat_arrival(t).wait_recv()
+    total = stats[0]
+    for s in range(1, tps):
+        total = total + stats[s]
+    inverse = lax.rsqrt(total / (part * tps) + EPSILON)
+
+    def start_own(r):
+        for way, can in ((0, z < floors - 1), (1, z > 0)):
+            pl.when(can)(lambda way=way: own(r, way).start())
+
+    for r in range(chunks):
+        line = jnp.broadcast_to(inverse[:, r * block : (r + 1) * block], (HEAD, block))
+        column = jnp.concatenate(
+            [jnp.transpose(line[:, b * HEAD : (b + 1) * HEAD]) for b in range(block // HEAD)], axis=0
+        )
+        column = jnp.concatenate([column] * (part // HEAD), axis=1)
+        place = (tp, pl.ds(r * block, block), slice(None))
+        acts[place] = (acts[place].astype(jnp.float32) * column * gain_ref[tp]).astype(jnp.bfloat16)
+        if r == 1:
+            link_event(0)
+        if r >= 1:
+            to_sibling(tp, r - 1).start()
+    link_event(1)
+    to_sibling(tp, chunks - 1).start()
+
+    lane = lax.broadcasted_iota(jnp.int32, (1, HEAD), 1)
+    sign = jnp.where(lane < HEAD // 2, -1.0, 1.0)
+
+    def table(first, count):
+        place = first + lax.broadcasted_iota(jnp.int32, (count, HEAD), 0)
+        angles = place.astype(jnp.float32) * freq_ref[...]
+        return jnp.cos(angles), jnp.sin(angles) * sign
+
+    def fill(b, _):
+        start = pl.multiple_of(b * HEAD, HEAD)
+        cand = joined * chunks + b // (block // HEAD)
+        cosines[pl.ds(start, HEAD), :], sines[pl.ds(start, HEAD), :] = table(
+            prefix_ref[cand] + b % (block // HEAD) * HEAD, HEAD
+        )
+        return 0
+
+    lax.fori_loop(0, rows // HEAD, fill, 0)
+
+    def rotated(value, cosine, sine):
+        return value * cosine + pltpu.roll(value, HEAD // 2, 1) * sine
+
+    pass_piece(0)
+    link_event(2)
+    send_piece(4)
+
+    load_p.wait()
+    slab_rows = 32
+
+    def norm_prompt(b, _):
+        where = pl.ds(pl.multiple_of(b * slab_rows, slab_rows), slab_rows)
+        squares = jnp.zeros((slab_rows, 1), jnp.float32)
+        for s in range(slices):
+            value = prompt[where, s * part : (s + 1) * part].astype(jnp.float32)
+            squares = squares + jnp.sum(value * value, axis=1, keepdims=True)
+        scale = lax.rsqrt(squares / (part * slices) + EPSILON)
+        for s in range(slices):
+            value = prompt[where, s * part : (s + 1) * part].astype(jnp.float32)
+            prompt[where, s * part : (s + 1) * part] = (value * scale * gain_ref[s]).astype(jnp.bfloat16)
+        return 0
+
+    lax.fori_loop(0, prompt_rows // slab_rows, norm_prompt, 0)
+    pass_piece(1)
+    link_event(3)
+    send_piece(5)
+    pass_piece(2)
+    link_event(4)
+
+    def await_piece(i):
+        place = piece_place(i, 1 - y, 1 - x)
+        pltpu.make_async_remote_copy(
+            src_ref=place, dst_ref=place, send_sem=rsend.at[i], recv_sem=rrecv.at[i],
+            device_id=aside, device_id_type=MESH,
+        ).wait_recv()
+
+    load_w[0].wait()
+    load_w[1].wait()
+    for i in range(2):
+        await_piece(i)
+
+    def prompt_block(b, _):
+        where = pl.ds(pl.multiple_of(b * HEAD, HEAD), HEAD)
+        product = jnp.dot(prompt[where, :part], wts[0, :part, :], preferred_element_type=jnp.float32)
+        for s in range(1, slices):
+            product = product + jnp.dot(
+                prompt[where, s * part : (s + 1) * part],
+                wts[0, s * part : (s + 1) * part, :],
+                preferred_element_type=jnp.float32,
+            )
+        cosine, sine = table(joined * prompt_rows + b * HEAD, HEAD)
+        kvp_ref[joined, where, :HEAD] = rotated(product[:, :HEAD] + kb_ref[...], cosine, sine).astype(jnp.bfloat16)
+        kvp_ref[joined, where, HEAD:] = (product[:, HEAD:] + vb_ref[...]).astype(jnp.bfloat16)
+        return 0
+
+    lax.fori_loop(0, prompt_rows // HEAD, prompt_block, 0)
+
+    def prompt_copy(n, slot):
+        return pltpu.make_async_remote_copy(
+            src_ref=kvp_ref.at[slot], dst_ref=kvp_ref.at[slot], send_sem=kp_send.at[n], recv_sem=kp_recv.at[n],
+            device_id=(over, aside, across)[n], device_id_type=MESH,
+        )
+
+    for n in range(3):
+        prompt_copy(n, joined).start()
+    for i in range(6, 8):
+        send_piece(i)
+    pass_piece(3)
+    link_event(5)
+    for i in range(8, pieces):
+        send_piece(i)
+
+    def await_columns(j):
+        load_w[2 + j].wait()
+        await_piece(2 + 2 * j)
+        await_piece(3 + 2 * j)
+
+    def await_chunk(r):
+        for f in range(floors):
+            to_sibling(2 * f + 1 - core, r).wait_recv()
+
+    plan = []
+    def add(events, *units):
+        for n, unit in enumerate(units):
+            plan.append((events if n == 0 else [], unit))
+
+    E, P, C, J = link_event, pass_piece, await_chunk, await_columns
+    add([(P, 4), (E, 6), (C, 0), (J, 0)], (0, 0), (0, 1))
+    add([(P, 5), (E, 7), (C, 1)], (1, 0), (1, 1))
+    add([(P, 6), (E, 8), (J, 1)], (0, 2), (1, 2))
+    add([(P, 7), (E, 9), (P, 8), (E, 10), (C, 2)], (2, 0), (2, 1), (2, 2))
+    add([(P, 9), (J, 2)], (0, 3), (1, 3), (2, 3))
+    add([(E, 11), (E, 12), (J, 3)], (0, 4), (1, 4), (2, 4))
+    add([(E, 13), (C, 3)], (3, 0), (3, 1), (3, 2), (3, 3), (3, 4))
+
+    def unit(u, _):
+        for k, (events, _unit) in enumerate(plan):
+            if events:
+
+                @pl.when(u == k)
+                def _():
+                    for call, argument in events:
+                        call(argument)
+
+        r, j = 0, 0
+        for k, (_events, (unit_r, unit_j)) in enumerate(plan):
+            r = r + jnp.where(u == k, unit_r, 0)
+            j = j + jnp.where(u == k, unit_j, 0)
+        where = pl.ds(pl.multiple_of(r * block, block), block)
+        product = jnp.dot(acts[0, where, :], wts[j, :part, :], preferred_element_type=jnp.float32)
+        for s in range(1, slices):
+            product = product + jnp.dot(
+                acts[s, where, :], wts[j, s * part : (s + 1) * part, :], preferred_element_type=jnp.float32
+            )
+        cosine, sine = cosines[where, :], sines[where, :]
+
+        @pl.when(j == 0)
+        def _():
+            kvc_ref[where, :HEAD] = rotated(product[:, :HEAD] + kb_ref[...], cosine, sine).astype(jnp.bfloat16)
+            kvc_ref[where, HEAD:] = (product[:, HEAD:] + vb_ref[...]).astype(jnp.bfloat16)
+
+        @pl.when(j > 0)
+        def _():
+            for h in range(2):
+                value = product[:, h * HEAD : (h + 1) * HEAD] + qb_ref[j - 1, :, h * HEAD : (h + 1) * HEAD]
+                q_ref[j - 1, where, h * HEAD : (h + 1) * HEAD] = rotated(value, cosine, sine).astype(jnp.bfloat16)
+
+        return 0
+
+    lax.fori_loop(0, len(plan), unit, 0)
+
+    for n, slot in enumerate(((1 - y) * 2 + x, y * 2 + 1 - x, (1 - y) * 2 + 1 - x)):
+        prompt_copy(n, slot).wait_recv()
+        prompt_copy(n, joined).wait_send()
+    for t in range(tps - 1):
+        stat_copy(t).wait_send()
+    for i in range(pieces):
+        direct(i).wait_send()
+        relay(i).wait_send()
+    for r in range(chunks):
+        to_sibling(tp, r).wait_send()
+        pl.when(z < floors - 1)(lambda: own(r, 0).wait_send())
+        pl.when(z > 0)(lambda: own(r, 1).wait_send())
+        for f in range(floors):
+            s = 2 * f + core
+
+            @pl.when(z != f)
+            def _():
+                to_sibling(s, r).wait_send()
+
+            @pl.when((f < z) & (z < floors - 1))
+            def _():
+                forward(s, r, up).wait_send()
+
+            @pl.when((f > z) & (z > 0))
+            def _():
+                forward(s, r, down).wait_send()
+
+
+def fits(prompt_inputs, cand_inputs, w_query, w_key):
+    rows, part = cand_inputs.shape
+    tps = lax.axis_size("tp")
+    return (
+        lax.axis_size("cache") == 2
+        and lax.axis_size("cand") == 2
+        and tps % 2 == 0
+        and tps >= 4
+        and rows == 4 * CLEN
+        and w_key.shape[1] == HEAD
+        and w_query.shape[1] == 8 * HEAD
+        and part * tps == D
+        and prompt_inputs.shape[0] % HEAD == 0
+        and prompt_inputs.shape[0] <= 4 * HEAD
+        and w_query.shape[0] == 4 * part
+    )
+
+
+def project(prompt_inputs, cand_inputs, norm_gain, w_query, w_key, w_value, q_bias, k_bias, v_bias, prefix_ends):
+    rows, part = cand_inputs.shape
+    tps = lax.axis_size("tp")
+    floors, chunks, wide = tps // 2, rows // CLEN, 2 * HEAD
+    columns = w_query.shape[1] // wide
+    pieces = 2 + 2 * columns
+    prompt_rows = prompt_inputs.shape[0]
+    half_freq = ROPE_THETA ** (-np.arange(HEAD // 2, dtype=np.float64) * 2.0 / HEAD)
+    freq = jnp.asarray(np.concatenate([half_freq, half_freq]).astype(np.float32).reshape(1, HEAD))
+    anywhere = pl.BlockSpec(memory_space=pl.ANY)
+    vmem = pl.BlockSpec(memory_space=pltpu.VMEM)
+    smem = pl.BlockSpec(memory_space=pltpu.SMEM)
+    dma = pltpu.SemaphoreType.DMA
+    return pl.pallas_call(
+        project_kernel,
+        out_shape=(
+            jax.ShapeDtypeStruct((columns, rows, wide), jnp.bfloat16),
+            jax.ShapeDtypeStruct((rows, wide), jnp.bfloat16),
+            jax.ShapeDtypeStruct((4, prompt_rows, wide), jnp.bfloat16),
+        ),
+        in_specs=[anywhere, anywhere, vmem, anywhere, anywhere, anywhere, vmem, vmem, vmem, vmem, smem],
+        out_specs=(vmem, vmem, vmem),
+        scratch_shapes=[
+            pltpu.VMEM((tps, rows, part), jnp.bfloat16),
+            pltpu.VMEM((1 + columns, part * tps, wide), jnp.bfloat16),
+            pltpu.VMEM((prompt_rows, part * tps), jnp.bfloat16),
+            pltpu.VMEM((rows, HEAD), jnp.float32),
+            pltpu.VMEM((rows, HEAD), jnp.float32),
+            pltpu.VMEM((tps, 1, rows), jnp.float32),
+            dma((4 + columns,)),
+            dma((pieces,)),
+            dma((pieces,)),
+            dma((pieces,)),
+            dma((pieces,)),
+            dma((2, chunks)),
+            dma((tps, chunks)),
+            dma((tps, chunks)),
+            dma((tps, chunks)),
+            dma((tps - 1,)),
+            dma((tps,)),
+            dma((3,)),
+            dma((3,)),
+        ],
+        compiler_params=pltpu.CompilerParams(
+            collective_id=0, has_side_effects=True, vmem_limit_bytes=64 * 1024 * 1024 - 65536
+        ),
+        name="project",
+    )(
+        cand_inputs.reshape(rows, part),
+        prompt_inputs,
+        norm_gain.reshape(tps, 1, part),
+        w_query,
+        w_key,
+        w_value,
+        q_bias.reshape(columns, 1, wide),
+        k_bias.reshape(1, HEAD),
+        v_bias.reshape(1, HEAD),
+        freq,
+        prefix_ends,
+    )
+
+
 def query_product(normed, w_query):
     caches = lax.axis_size("cache")
     cands = lax.axis_size("cand")
@@ -191,6 +664,21 @@
     groups = HEADS // KV_HEADS
     kv_width = kv_local * head_size
     joined = lax.axis_index("cache") * lax.axis_size("cand") + lax.axis_index("cand")
+    if fits(prompt_inputs, cand_inputs, w_query, w_key):
+        q_cand, kv_c, kv_p = project(
+            prompt_inputs, cand_inputs, norm_gain, w_query, w_key, w_value, q_bias, k_bias, v_bias, prefix_ends
+        )
+        tile_first = joined * cand_dev + CLEN * jnp.arange(cand_dev // CLEN, dtype=jnp.int32)
+        return attend(
+            row_lookup(tile_first, prefix_ends),
+            row_lookup(tile_first, cand_lengths),
+            tile_first % CLEN,
+            q_cand.transpose(1, 0, 2).reshape(cand_dev, -1),
+            kv_p.reshape(-1, 2 * kv_width),
+            kv_c,
+            kv_local,
+            groups,
+        )
     widened_p = prompt_inputs.astype(jnp.float32)
     normed_p = (
         widened_p

time: 352 us -> 214 us (0.61)
  the two profiles are of different devices: /device:TPU:0 before, /device:TPU:5 now
where the time goes in v1:
time: 214 us; the launch traced here: 212 us
  Pallas kernels  207 us (97%)
  local copies, waits for them, and re-layouts  3.23 us (2%)
    pallas_call x1, Pallas kernels, project(): pl.pallas_call(project_kernel, out_shape=(jax.ShapeDtypeStruct((columns,...  158 us
    pallas_call x1, Pallas kernels, attend(): pl.pallas_call(functools.partial(attend_kernel, heads=heads, chunk=chunk,...  49.3 us

profile of v1, /device:TPU:5, one launch (start us, length us, event | category | flops | bytes accessed | tf_op | source)
XLA Modules:
  0.0 212.2 jit_solution(4820099513391643587)
XLA Ops:
  0.0 0.5 and_select_fusion
  0.5 1.4 select_reduce_fusion
  1.9 157.8 %project.1 = (bf16[4,1024,256]{2,1,0:T(8,128)(2,1)}, bf16[1024,256]{1,0:T(8,128)(2,1)}, bf16[4,384,256]{2,1,0:T(8,128)(2,1)}) custom-call(bf16[1024,1024]{1,0:T(8,128)(2,1)} %xc_ref.1, bf16[384,8192]{1,0:T(8,128)(2,1)} %xp_ref.1, f32[8,1,1024]{2,1,0:T(1,128)} %bitcast.10, bf16[4096,1024]{1,0:T(8,128)(2,1)} %wq_ref.1, bf16[4096,128]{1,0:T(8,128)(2,1)} %wk_ref.1, ...), custom_call_target="tpu_custom_call" | custom-call | tf_op jit(solution)/shard_map/project/pallas_call | solution.py:563
  159.7 3.2 %copy.15 = bf16[4,128,8,256]{3,2,0,1:T(8,128)(2,1)} copy(bf16[4,128,8,256]{3,2,1,0:T(8,128)(2,1)} %bitcast.9) | data formatting | bytes 4194304 | tf_op jit(solution)/shard_map/reshape | solution.py:676
  162.9 49.3 %shard_map.118 = bf16[1024,1024]{1,0:T(8,128)(2,1)} custom-call(s32[4]{0:T(128)} %get-tuple-element.12.prefix_ref, s32[4]{0:T(128)} %get-tuple-element.11.length_ref, s32[4]{0:T(128)} %get-tuple-element.13.offset_ref, bf16[1024,1024]{1,0:T(8,128)(2,1)} %bitcast.8, bf16[1536,256]{1,0:T(8,128)(2,1)} %bitcast.14, bf16[1024,256]{1,0:T(8,128)(2,1)} %get-tuple-element.10.kvc_ref), custom_call_target="tpu_custom_call" | custom-call | flops 7516192768 | bytes 4194304 | tf_op jit(solution)/shard_map/pallas_call | solution.py:116

commit v2 on v1

--- a/solution.py
+++ b/solution.py
@@ -156,11 +156,11 @@
     return orders
 
 
-def project_kernel(
-    xc_ref, xp_ref, gain_ref, wq_ref, wk_ref, wv_ref, qb_ref, kb_ref, vb_ref, freq_ref, prefix_ref,
-    q_ref, kvc_ref, kvp_ref,
-    acts, wts, prompt, cosines, sines, stats,
-    load_sem, wsend, wrecv, rsend, rrecv, own_sem, fwd_sem, sib_sem, arr_sem, st_send, st_recv, kp_send, kp_recv,
+def layer_kernel(
+    xc_ref, xp_ref, gain_ref, wq_ref, wk_ref, wv_ref, qb_ref, kb_ref, vb_ref, freq_ref, prefix_ref, length_ref,
+    out_ref,
+    acts, wts, prompt, cosines, sines, stats, keys_p, values_p, keys_c, values_c, hidden, scores, results,
+    load_sem, wsend, wrecv, rsend, rrecv, own_sem, fwd_sem, sib_sem, arr_sem, st_send, st_recv, kp_send, kp_recv, out_sem,
 ):
     y, tp, x = lax.axis_index("cache"), lax.axis_index("tp"), lax.axis_index("cand")
     tps = lax.axis_size("tp")
@@ -370,6 +370,16 @@
 
     lax.fori_loop(0, rows // HEAD, fill, 0)
 
+    def hide(n, _):
+        r, b = n // 4, n % 4
+        key = b * prompt_rows + lax.broadcasted_iota(jnp.int32, (prompt_rows, HEAD), 0)
+        first = lax.broadcasted_iota(jnp.int32, (prompt_rows, HEAD), 1) == 0
+        unseen = first & (key >= prefix_ref[joined * chunks + r])
+        hidden[r, b] = jnp.where(unseen, -1e30, 0.0).astype(jnp.bfloat16)
+        return 0
+
+    lax.fori_loop(0, 4 * chunks, hide, 0)
+
     def rotated(value, cosine, sine):
         return value * cosine + pltpu.roll(value, HEAD // 2, 1) * sine
 
@@ -421,20 +431,22 @@
                 preferred_element_type=jnp.float32,
             )
         cosine, sine = table(joined * prompt_rows + b * HEAD, HEAD)
-        kvp_ref[joined, where, :HEAD] = rotated(product[:, :HEAD] + kb_ref[...], cosine, sine).astype(jnp.bfloat16)
-        kvp_ref[joined, where, HEAD:] = (product[:, HEAD:] + vb_ref[...]).astype(jnp.bfloat16)
+        keys_p[joined, where, :] = rotated(product[:, :HEAD] + kb_ref[...], cosine, sine).astype(jnp.bfloat16)
+        values_p[joined, :, where] = jnp.transpose(product[:, HEAD:] + vb_ref[...]).astype(jnp.bfloat16)
         return 0
 
     lax.fori_loop(0, prompt_rows // HEAD, prompt_block, 0)
 
-    def prompt_copy(n, slot):
+    def prompt_copy(n, kind, slot):
+        place = (keys_p, values_p)[kind].at[slot]
         return pltpu.make_async_remote_copy(
-            src_ref=kvp_ref.at[slot], dst_ref=kvp_ref.at[slot], send_sem=kp_send.at[n], recv_sem=kp_recv.at[n],
+            src_ref=place, dst_ref=place, send_sem=kp_send.at[n, kind], recv_sem=kp_recv.at[n, kind],
             device_id=(over, aside, across)[n], device_id_type=MESH,
         )
 
     for n in range(3):
-        prompt_copy(n, joined).start()
+        for kind in range(2):
+            prompt_copy(n, kind, joined).start()
     for i in range(6, 8):
         send_piece(i)
     pass_piece(3)
@@ -451,13 +463,83 @@
         for f in range(floors):
             to_sibling(2 * f + 1 - core, r).wait_recv()
 
+    def await_prompt(_):
+        for n, slot in enumerate(((1 - y) * 2 + x, y * 2 + 1 - x, (1 - y) * 2 + 1 - x)):
+            for kind in range(2):
+                prompt_copy(n, kind, slot).wait_recv()
+
+    def result_copy(r, j):
+        where = pl.ds(pl.multiple_of(r * block, block), block)
+        across_columns = pl.ds(pl.multiple_of(j * wide, wide), wide)
+        return pltpu.make_async_copy(
+            results.at[j, where, :], out_ref.at[where, across_columns], out_sem.at[r, j]
+        )
+
+    def attend_heads(r, queries, write):
+        extra = jnp.where(lax.broadcasted_iota(jnp.int32, (block, HEAD), 1) == 0, 1.0, 0.0).astype(jnp.bfloat16)
+        own_keys = pl.ds(pl.multiple_of(r * block, block), block)
+        contract = (((1,), (1,)), ((), ()))
+        states = [{} for _ in queries]
+        factor = HEAD ** (-0.5) * math.log2(math.e)
+
+        def span(b):
+            return slice(b * prompt_rows, (b + 1) * prompt_rows if b < 4 else 4 * prompt_rows + block)
+
+        def score(h, b):
+            state = states[h]
+            if b < 4:
+                found = lax.dot_general(
+                    jnp.concatenate([keys_p[b], hidden[r, b]], axis=1),
+                    jnp.concatenate([queries[h], extra], axis=1),
+                    contract,
+                    preferred_element_type=jnp.float32,
+                )
+            else:
+                found = lax.dot_general(
+                    keys_c[own_keys, :], queries[h], contract, preferred_element_type=jnp.float32
+                )
+                shape = (block, block)
+                found = jnp.where(
+                    lax.broadcasted_iota(jnp.int32, shape, 0) <= lax.broadcasted_iota(jnp.int32, shape, 1), found, -1e30
+                )
+            scores[h, span(b), :] = found
+            highest = jnp.max(found.reshape(-1, 8, block), axis=0)
+            state["max"] = jnp.maximum(state["max"], highest) if "max" in state else highest
+            if b == 4:
+                state["max"] = jnp.max(state["max"], axis=0, keepdims=True) * factor
+
+        def weigh(h, b):
+            state = states[h]
+            chances = jnp.exp2(scores[h, span(b), :] * factor - state["max"])
+            total = jnp.sum(chances.reshape(-1, 8, block), axis=0)
+            values = values_p[b] if b < 4 else values_c[:, own_keys]
+            mixed = jnp.dot(values, chances.astype(jnp.bfloat16), preferred_element_type=jnp.float32)
+            state["sum"] = state["sum"] + total if "sum" in state else total
+            state["mix"] = state["mix"] + mixed if "mix" in state else mixed
+
+        def finish(h):
+            state = states[h]
+            result = jnp.transpose(state["mix"] / jnp.sum(state["sum"], axis=0, keepdims=True))
+            valid = lax.broadcasted_iota(jnp.int32, (block, HEAD), 0) < length_ref[joined * chunks + r]
+            write(h, jnp.where(valid, result, 0.0).astype(jnp.bfloat16))
+
+        for b in range(5):
+            score(0, b)
+        for b in range(5):
+            weigh(0, b)
+            score(1, b)
+        finish(0)
+        for b in range(5):
+            weigh(1, b)
+        finish(1)
+
     plan = []
     def add(events, *units):
         for n, unit in enumerate(units):
             plan.append((events if n == 0 else [], unit))
 
     E, P, C, J = link_event, pass_piece, await_chunk, await_columns
-    add([(P, 4), (E, 6), (C, 0), (J, 0)], (0, 0), (0, 1))
+    add([(P, 4), (E, 6), (C, 0), (J, 0), (await_prompt, 0)], (0, 0), (0, 1))
     add([(P, 5), (E, 7), (C, 1)], (1, 0), (1, 1))
     add([(P, 6), (E, 8), (J, 1)], (0, 2), (1, 2))
     add([(P, 7), (E, 9), (P, 8), (E, 10), (C, 2)], (2, 0), (2, 1), (2, 2))
@@ -488,22 +570,36 @@
 
         @pl.when(j == 0)
         def _():
-            kvc_ref[where, :HEAD] = rotated(product[:, :HEAD] + kb_ref[...], cosine, sine).astype(jnp.bfloat16)
-            kvc_ref[where, HEAD:] = (product[:, HEAD:] + vb_ref[...]).astype(jnp.bfloat16)
+            keys_c[where, :] = rotated(product[:, :HEAD] + kb_ref[...], cosine, sine).astype(jnp.bfloat16)
+            turned = product[:, HEAD:] + vb_ref[...]
+            for b in range(block // HEAD):
+                values_c[:, pl.ds(pl.multiple_of(r * block + b * HEAD, HEAD), HEAD)] = jnp.transpose(
+                    turned[b * HEAD : (b + 1) * HEAD, :]
+                ).astype(jnp.bfloat16)
 
         @pl.when(j > 0)
         def _():
+            queries = []
             for h in range(2):
                 value = product[:, h * HEAD : (h + 1) * HEAD] + qb_ref[j - 1, :, h * HEAD : (h + 1) * HEAD]
-                q_ref[j - 1, where, h * HEAD : (h + 1) * HEAD] = rotated(value, cosine, sine).astype(jnp.bfloat16)
+                queries.append(rotated(value, cosine, sine).astype(jnp.bfloat16))
+
+            def write(h, value):
+                results[j - 1, where, h * HEAD : (h + 1) * HEAD] = value
+
+            attend_heads(r, queries, write)
+            result_copy(r, j - 1).start()
 
         return 0
 
     lax.fori_loop(0, len(plan), unit, 0)
 
-    for n, slot in enumerate(((1 - y) * 2 + x, y * 2 + 1 - x, (1 - y) * 2 + 1 - x)):
-        prompt_copy(n, slot).wait_recv()
-        prompt_copy(n, joined).wait_send()
+    for r in range(chunks):
+        for j in range(columns):
+            result_copy(r, j).wait()
+    for n in range(3):
+        for kind in range(2):
+            prompt_copy(n, kind, joined).wait_send()
     for t in range(tps - 1):
         stat_copy(t).wait_send()
     for i in range(pieces):
@@ -547,7 +643,19 @@
     )
 
 
-def project(prompt_inputs, cand_inputs, norm_gain, w_query, w_key, w_value, q_bias, k_bias, v_bias, prefix_ends):
+def whole_layer(
+    prompt_inputs,
+    cand_inputs,
+    norm_gain,
+    w_query,
+    w_key,
+    w_value,
+    q_bias,
+    k_bias,
+    v_bias,
+    cand_lengths,
+    prefix_ends,
+):
     rows, part = cand_inputs.shape
     tps = lax.axis_size("tp")
     floors, chunks, wide = tps // 2, rows // CLEN, 2 * HEAD
@@ -561,14 +669,10 @@
     smem = pl.BlockSpec(memory_space=pltpu.SMEM)
     dma = pltpu.SemaphoreType.DMA
     return pl.pallas_call(
-        project_kernel,
-        out_shape=(
-            jax.ShapeDtypeStruct((columns, rows, wide), jnp.bfloat16),
-            jax.ShapeDtypeStruct((rows, wide), jnp.bfloat16),
-            jax.ShapeDtypeStruct((4, prompt_rows, wide), jnp.bfloat16),
-        ),
-        in_specs=[anywhere, anywhere, vmem, anywhere, anywhere, anywhere, vmem, vmem, vmem, vmem, smem],
-        out_specs=(vmem, vmem, vmem),
+        layer_kernel,
+        out_shape=jax.ShapeDtypeStruct((rows, columns * wide), jnp.bfloat16),
+        in_specs=[anywhere, anywhere, vmem, anywhere, anywhere, anywhere, vmem, vmem, vmem, vmem, smem, smem],
+        out_specs=anywhere,
         scratch_shapes=[
             pltpu.VMEM((tps, rows, part), jnp.bfloat16),
             pltpu.VMEM((1 + columns, part * tps, wide), jnp.bfloat16),
@@ -576,6 +680,13 @@
             pltpu.VMEM((rows, HEAD), jnp.float32),
             pltpu.VMEM((rows, HEAD), jnp.float32),
             pltpu.VMEM((tps, 1, rows), jnp.float32),
+            pltpu.VMEM((4, prompt_rows, HEAD), jnp.bfloat16),
+            pltpu.VMEM((4, HEAD, prompt_rows), jnp.bfloat16),
+            pltpu.VMEM((rows, HEAD), jnp.bfloat16),
+            pltpu.VMEM((HEAD, rows), jnp.bfloat16),
+            pltpu.VMEM((chunks, 4, prompt_rows, HEAD), jnp.bfloat16),
+            pltpu.VMEM((2, 4 * prompt_rows + CLEN, CLEN), jnp.float32),
+            pltpu.VMEM((columns, rows, wide), jnp.bfloat16),
             dma((4 + columns,)),
             dma((pieces,)),
             dma((pieces,)),
@@ -587,13 +698,14 @@
             dma((tps, chunks)),
             dma((tps - 1,)),
             dma((tps,)),
-            dma((3,)),
-            dma((3,)),
+            dma((3, 2)),
+            dma((3, 2)),
+            dma((chunks, columns)),
         ],
         compiler_params=pltpu.CompilerParams(
             collective_id=0, has_side_effects=True, vmem_limit_bytes=64 * 1024 * 1024 - 65536
         ),
-        name="project",
+        name="whole_layer",
     )(
         cand_inputs.reshape(rows, part),
         prompt_inputs,
@@ -606,6 +718,7 @@
         v_bias.reshape(1, HEAD),
         freq,
         prefix_ends,
+        cand_lengths,
     )
 
 
@@ -665,19 +778,18 @@
     kv_width = kv_local * head_size
     joined = lax.axis_index("cache") * lax.axis_size("cand") + lax.axis_index("cand")
     if fits(prompt_inputs, cand_inputs, w_query, w_key):
-        q_cand, kv_c, kv_p = project(
-            prompt_inputs, cand_inputs, norm_gain, w_query, w_key, w_value, q_bias, k_bias, v_bias, prefix_ends
-        )
-        tile_first = joined * cand_dev + CLEN * jnp.arange(cand_dev // CLEN, dtype=jnp.int32)
-        return attend(
-            row_lookup(tile_first, prefix_ends),
-            row_lookup(tile_first, cand_lengths),
-            tile_first % CLEN,
-            q_cand.transpose(1, 0, 2).reshape(cand_dev, -1),
-            kv_p.reshape(-1, 2 * kv_width),
-            kv_c,
-            kv_local,
-            groups,
+        return whole_layer(
+            prompt_inputs,
+            cand_inputs,
+            norm_gain,
+            w_query,
+            w_key,
+            w_value,
+            q_bias,
+            k_bias,
+            v_bias,
+            cand_lengths,
+            prefix_ends,
         )
     widened_p = prompt_inputs.astype(jnp.float32)
     normed_p = (

time: 214 us -> 180 us (0.84)
  the two profiles are of different devices: /device:TPU:5 before, /device:TPU:0 now
where the time goes in v2:
time: 180 us; the launch traced here: 178 us
  Pallas kernels  175 us (97%)
  local copies, waits for them, and re-layouts  3.08 us (2%)
    pallas_call x1, Pallas kernels, whole_layer(): pl.pallas_call(layer_kernel, out_shape=jax.ShapeDtypeStruct((rows, column...  175 us

profile of v2, /device:TPU:0, one launch (start us, length us, event | category | flops | bytes accessed | tf_op | source)
XLA Modules:
  0.0 178.1 jit_solution(6649626027332861727)
XLA Ops:
  0.0 175.0 %whole_layer.1 = bf16[1024,1024]{1,0:T(8,128)(2,1)} custom-call(bf16[1024,1024]{1,0:T(8,128)(2,1)} %xc_ref.1, bf16[384,8192]{1,0:T(8,128)(2,1)} %xp_ref.1, f32[8,1,1024]{2,1,0:T(1,128)} %bitcast.4, bf16[4096,1024]{1,0:T(8,128)(2,1)} %wq_ref.1, bf16[4096,128]{1,0:T(8,128)(2,1)} %wk_ref.1, bf16[4096,128]{1,0:T(8,128)(2,1)} %wv_ref.1, f32[4,1,256]{2,1,0:T(1,128)} %bitcast.5, ...), custom_call_target="tpu_custom_call" | custom-call | tf_op jit(solution)/shard_map/whole_layer/pallas_call | solution.py:671
  175.0 3.1 %copy.14 = bf16[1024,1024]{1,0:T(8,128)(2,1)} copy(bf16[1024,1024]{1,0:T(8,128)(2,1)} %whole_layer.1) | data formatting | bytes 4194304

commit v3 on v2

--- a/solution.py
+++ b/solution.py
@@ -140,6 +140,19 @@
 MESH = pl.DeviceIdType.MESH
 
 
+def chunk_bounds(rows):
+    whole = [(first, CLEN) for first in range(0, rows - CLEN, CLEN)]
+    return whole + [(rows - CLEN, CLEN // 2), (rows - CLEN // 2, CLEN // 2)]
+
+
+def piece_table(columns, quarter):
+    table = [(0, 0, quarter), (0, 0, quarter)]
+    for j in range(columns):
+        count = 2 if j < columns - 1 else 4
+        table += [(1 + j, n * (quarter // count), quarter // count) for n in range(count)]
+    return table
+
+
 def link_orders(depths, chunks):
     orders = [[(0, r) for r in range(chunks)]]
     for depth in range(1, depths):
@@ -168,13 +181,15 @@
     z, core = tp // 2, tp % 2
     rows, part = xc_ref.shape
     block = CLEN
-    chunks = rows // block
+    cands = rows // block
+    bounds = chunk_bounds(rows)
+    chunks = len(bounds)
     half = wq_ref.shape[0]
     quarter = half // 2
-    piece_rows = quarter // 2
     wide = 2 * HEAD
     columns = wq_ref.shape[1] // wide
-    pieces = 2 + 2 * columns
+    table_of_pieces = piece_table(columns, quarter)
+    pieces = len(table_of_pieces)
     prompt_rows = xp_ref.shape[0]
     slices = tps
     joined = y * 2 + x
@@ -205,21 +220,14 @@
         copy.start()
 
     def piece_place(i, side_y, side_x):
-        base = side_y * half + side_x * quarter
-        if i < 2:
-            where = pl.ds(pl.multiple_of(base, quarter), quarter)
-            return wts.at[0, where, i * HEAD : (i + 1) * HEAD]
-        j, h = divmod(i - 2, 2)
-        where = pl.ds(pl.multiple_of(base + h * piece_rows, piece_rows), piece_rows)
-        return wts.at[1 + j, where, :]
+        j, first, count = table_of_pieces[i]
+        where = pl.ds(pl.multiple_of(side_y * half + side_x * quarter + first, count), count)
+        return wts.at[0, where, i * HEAD : (i + 1) * HEAD] if j == 0 else wts.at[j, where, :]
 
     def direct(i):
-        if i < 2:
-            src = (wk_ref, wv_ref)[i].at[pl.ds(pl.multiple_of(x * quarter, quarter), quarter), :]
-        else:
-            j, h = divmod(i - 2, 2)
-            where = pl.ds(pl.multiple_of(x * quarter + h * piece_rows, piece_rows), piece_rows)
-            src = wq_ref.at[where, j * wide : (j + 1) * wide]
+        j, first, count = table_of_pieces[i]
+        where = pl.ds(pl.multiple_of(x * quarter + first, count), count)
+        src = (wk_ref, wv_ref)[i].at[where, :] if j == 0 else wq_ref.at[where, (j - 1) * wide : j * wide]
         return pltpu.make_async_remote_copy(
             src_ref=src, dst_ref=piece_place(i, y, x), send_sem=wsend.at[i], recv_sem=wrecv.at[i],
             device_id=over, device_id_type=MESH,
@@ -242,7 +250,7 @@
             direct(i).start()
 
     def slab(s, r):
-        return acts.at[s, pl.ds(r * block, block), :]
+        return acts.at[s, pl.ds(*bounds[r]), :]
 
     def slab_copy(s, r, send, target):
         return pltpu.make_async_remote_copy(
@@ -297,7 +305,7 @@
             pl.when(floors - 1 - z == depth)(functools.partial(go, 1, 1, down))
 
     load_x.wait()
-    for r in range(chunks):
+    for r in range(cands):
         wide_x = acts[tp, pl.ds(r * block, block), :].astype(jnp.float32)
         squares = wide_x * wide_x
         lanes = squares[:, :HEAD]
@@ -333,11 +341,7 @@
         total = total + stats[s]
     inverse = lax.rsqrt(total / (part * tps) + EPSILON)
 
-    def start_own(r):
-        for way, can in ((0, z < floors - 1), (1, z > 0)):
-            pl.when(can)(lambda way=way: own(r, way).start())
-
-    for r in range(chunks):
+    for r in range(cands):
         line = jnp.broadcast_to(inverse[:, r * block : (r + 1) * block], (HEAD, block))
         column = jnp.concatenate(
             [jnp.transpose(line[:, b * HEAD : (b + 1) * HEAD]) for b in range(block // HEAD)], axis=0
@@ -350,7 +354,8 @@
         if r >= 1:
             to_sibling(tp, r - 1).start()
     link_event(1)
-    to_sibling(tp, chunks - 1).start()
+    for r in range(cands - 1, chunks):
+        to_sibling(tp, r).start()
 
     lane = lax.broadcasted_iota(jnp.int32, (1, HEAD), 1)
     sign = jnp.where(lane < HEAD // 2, -1.0, 1.0)
@@ -362,7 +367,7 @@
 
     def fill(b, _):
         start = pl.multiple_of(b * HEAD, HEAD)
-        cand = joined * chunks + b // (block // HEAD)
+        cand = joined * cands + b // (block // HEAD)
         cosines[pl.ds(start, HEAD), :], sines[pl.ds(start, HEAD), :] = table(
             prefix_ref[cand] + b % (block // HEAD) * HEAD, HEAD
         )
@@ -374,18 +379,20 @@
         r, b = n // 4, n % 4
         key = b * prompt_rows + lax.broadcasted_iota(jnp.int32, (prompt_rows, HEAD), 0)
         first = lax.broadcasted_iota(jnp.int32, (prompt_rows, HEAD), 1) == 0
-        unseen = first & (key >= prefix_ref[joined * chunks + r])
+        unseen = first & (key >= prefix_ref[joined * cands + r])
         hidden[r, b] = jnp.where(unseen, -1e30, 0.0).astype(jnp.bfloat16)
         return 0
 
-    lax.fori_loop(0, 4 * chunks, hide, 0)
+    lax.fori_loop(0, 4 * cands, hide, 0)
+    later = pl.ds(*bounds[-1])
+    keys_c[later, :] = jnp.zeros((bounds[-1][1], HEAD), jnp.bfloat16)
+    values_c[:, later] = jnp.zeros((HEAD, bounds[-1][1]), jnp.bfloat16)
 
     def rotated(value, cosine, sine):
         return value * cosine + pltpu.roll(value, HEAD // 2, 1) * sine
 
     pass_piece(0)
     link_event(2)
-    send_piece(4)
 
     load_p.wait()
     slab_rows = 32
@@ -405,7 +412,6 @@
     lax.fori_loop(0, prompt_rows // slab_rows, norm_prompt, 0)
     pass_piece(1)
     link_event(3)
-    send_piece(5)
     pass_piece(2)
     link_event(4)
 
@@ -447,17 +453,18 @@
     for n in range(3):
         for kind in range(2):
             prompt_copy(n, kind, joined).start()
-    for i in range(6, 8):
+    for i in range(4, 7):
         send_piece(i)
     pass_piece(3)
     link_event(5)
-    for i in range(8, pieces):
+    for i in range(7, pieces):
         send_piece(i)
 
     def await_columns(j):
         load_w[2 + j].wait()
-        await_piece(2 + 2 * j)
-        await_piece(3 + 2 * j)
+        for i in range(2, pieces):
+            if table_of_pieces[i][0] == 1 + j:
+                await_piece(i)
 
     def await_chunk(r):
         for f in range(floors):
@@ -468,19 +475,23 @@
             for kind in range(2):
                 prompt_copy(n, kind, slot).wait_recv()
 
-    def result_copy(r, j):
-        where = pl.ds(pl.multiple_of(r * block, block), block)
+    def result_copy(n, j):
+        where = pl.ds(*bounds[n]) if isinstance(n, int) else pl.ds(pl.multiple_of(n * block, block), block)
+        return result_place(n, j, where)
+
+    def result_place(n, j, where):
         across_columns = pl.ds(pl.multiple_of(j * wide, wide), wide)
         return pltpu.make_async_copy(
-            results.at[j, where, :], out_ref.at[where, across_columns], out_sem.at[r, j]
-        )
-
-    def attend_heads(r, queries, write):
+            results.at[j, where, :], out_ref.at[where, across_columns], out_sem.at[n, j]
+        )
+
+    factor = HEAD ** (-0.5) * math.log2(math.e)
+
+    def attend_heads(r, own_rows, queries, valid, write):
         extra = jnp.where(lax.broadcasted_iota(jnp.int32, (block, HEAD), 1) == 0, 1.0, 0.0).astype(jnp.bfloat16)
         own_keys = pl.ds(pl.multiple_of(r * block, block), block)
         contract = (((1,), (1,)), ((), ()))
         states = [{} for _ in queries]
-        factor = HEAD ** (-0.5) * math.log2(math.e)
 
         def span(b):
             return slice(b * prompt_rows, (b + 1) * prompt_rows if b < 4 else 4 * prompt_rows + block)
@@ -498,10 +509,7 @@
                 found = lax.dot_general(
                     keys_c[own_keys, :], queries[h], contract, preferred_element_type=jnp.float32
                 )
-                shape = (block, block)
-                found = jnp.where(
-                    lax.broadcasted_iota(jnp.int32, shape, 0) <= lax.broadcasted_iota(jnp.int32, shape, 1), found, -1e30
-                )
+                found = jnp.where(lax.broadcasted_iota(jnp.int32, (block, block), 0) <= own_rows, found, -1e30)
             scores[h, span(b), :] = found
             highest = jnp.max(found.reshape(-1, 8, block), axis=0)
             state["max"] = jnp.maximum(state["max"], highest) if "max" in state else highest
@@ -520,76 +528,120 @@
         def finish(h):
             state = states[h]
             result = jnp.transpose(state["mix"] / jnp.sum(state["sum"], axis=0, keepdims=True))
-            valid = lax.broadcasted_iota(jnp.int32, (block, HEAD), 0) < length_ref[joined * chunks + r]
             write(h, jnp.where(valid, result, 0.0).astype(jnp.bfloat16))
 
+        count = len(queries)
         for b in range(5):
             score(0, b)
-        for b in range(5):
-            weigh(0, b)
-            score(1, b)
-        finish(0)
-        for b in range(5):
-            weigh(1, b)
-        finish(1)
-
-    plan = []
-    def add(events, *units):
-        for n, unit in enumerate(units):
-            plan.append((events if n == 0 else [], unit))
-
-    E, P, C, J = link_event, pass_piece, await_chunk, await_columns
-    add([(P, 4), (E, 6), (C, 0), (J, 0), (await_prompt, 0)], (0, 0), (0, 1))
-    add([(P, 5), (E, 7), (C, 1)], (1, 0), (1, 1))
-    add([(P, 6), (E, 8), (J, 1)], (0, 2), (1, 2))
-    add([(P, 7), (E, 9), (P, 8), (E, 10), (C, 2)], (2, 0), (2, 1), (2, 2))
-    add([(P, 9), (J, 2)], (0, 3), (1, 3), (2, 3))
-    add([(E, 11), (E, 12), (J, 3)], (0, 4), (1, 4), (2, 4))
-    add([(E, 13), (C, 3)], (3, 0), (3, 1), (3, 2), (3, 3), (3, 4))
-
-    def unit(u, _):
-        for k, (events, _unit) in enumerate(plan):
-            if events:
-
-                @pl.when(u == k)
-                def _():
-                    for call, argument in events:
-                        call(argument)
-
-        r, j = 0, 0
-        for k, (_events, (unit_r, unit_j)) in enumerate(plan):
-            r = r + jnp.where(u == k, unit_r, 0)
-            j = j + jnp.where(u == k, unit_j, 0)
-        where = pl.ds(pl.multiple_of(r * block, block), block)
+        for h in range(count):
+            for b in range(5):
+                weigh(h, b)
+                if h + 1 < count:
+                    score(h + 1, b)
+            finish(h)
+
+    def projected(where, j):
         product = jnp.dot(acts[0, where, :], wts[j, :part, :], preferred_element_type=jnp.float32)
         for s in range(1, slices):
             product = product + jnp.dot(
                 acts[s, where, :], wts[j, s * part : (s + 1) * part, :], preferred_element_type=jnp.float32
             )
+        return product
+
+    def keep_keys(first, count, product, cosine, sine):
+        keys_c[pl.ds(first, count), :] = rotated(product[:, :HEAD] + kb_ref[...], cosine, sine).astype(jnp.bfloat16)
+        turned = product[:, HEAD:] + vb_ref[...]
+        for b in range(count // HEAD):
+            values_c[:, pl.ds(pl.multiple_of(first + b * HEAD, HEAD), HEAD)] = jnp.transpose(
+                turned[b * HEAD : (b + 1) * HEAD, :]
+            ).astype(jnp.bfloat16)
+
+    def queries_of(j, product, cosine, sine):
+        found = []
+        for h in range(2):
+            value = product[:, h * HEAD : (h + 1) * HEAD] + qb_ref[j - 1, :, h * HEAD : (h + 1) * HEAD]
+            found.append(rotated(value, cosine, sine).astype(jnp.bfloat16))
+        return found
+
+    def whole_unit(r, j):
+        first = pl.multiple_of(r * block, block)
+        where = pl.ds(first, block)
+        product = projected(where, j)
         cosine, sine = cosines[where, :], sines[where, :]
-
-        @pl.when(j == 0)
-        def _():
-            keys_c[where, :] = rotated(product[:, :HEAD] + kb_ref[...], cosine, sine).astype(jnp.bfloat16)
-            turned = product[:, HEAD:] + vb_ref[...]
-            for b in range(block // HEAD):
-                values_c[:, pl.ds(pl.multiple_of(r * block + b * HEAD, HEAD), HEAD)] = jnp.transpose(
-                    turned[b * HEAD : (b + 1) * HEAD, :]
-                ).astype(jnp.bfloat16)
+        pl.when(j == 0)(lambda: keep_keys(first, block, product, cosine, sine))
 
         @pl.when(j > 0)
         def _():
-            queries = []
-            for h in range(2):
-                value = product[:, h * HEAD : (h + 1) * HEAD] + qb_ref[j - 1, :, h * HEAD : (h + 1) * HEAD]
-                queries.append(rotated(value, cosine, sine).astype(jnp.bfloat16))
+            queries = queries_of(j, product, cosine, sine)
 
             def write(h, value):
                 results[j - 1, where, h * HEAD : (h + 1) * HEAD] = value
 
-            attend_heads(r, queries, write)
+            valid = lax.broadcasted_iota(jnp.int32, (block, HEAD), 0) < length_ref[joined * cands + r]
+            attend_heads(r, lax.broadcasted_iota(jnp.int32, (block, block), 1), queries, valid, write)
             result_copy(r, j - 1).start()
 
+    def half_unit(n, j):
+        count = block // 2
+        r = cands - 1
+        offset = (n - r) * count
+        first = pl.multiple_of(r * block + offset, count)
+        where = pl.ds(first, count)
+        product = projected(where, j)
+        cosine, sine = cosines[where, :], sines[where, :]
+        pl.when(j == 0)(lambda: keep_keys(first, count, product, cosine, sine))
+
+        @pl.when(j > 0)
+        def _():
+            queries = jnp.concatenate(queries_of(j, product, cosine, sine), axis=0)
+
+            def write(_h, value):
+                for h in range(2):
+                    results[j - 1, where, h * HEAD : (h + 1) * HEAD] = value[h * count : (h + 1) * count, :]
+
+            def own_row(axis, shape):
+                place = lax.broadcasted_iota(jnp.int32, shape, axis)
+                return offset + jnp.where(place < count, place, place - count)
+
+            valid = own_row(0, (block, HEAD)) < length_ref[joined * cands + r]
+            attend_heads(r, own_row(1, (block, block)), [queries], valid, write)
+            result_place(n, j - 1, where).start()
+
+    plan = []
+
+    def add(events, *units):
+        for n, unit in enumerate(units):
+            plan.append((events if n == 0 else [], unit))
+
+    E, P, C, J = link_event, pass_piece, await_chunk, await_columns
+    add([(E, 6), (P, 4), (C, 0), (J, 0), (await_prompt, 0)], (0, 0), (0, 1))
+    add([(E, 7), (C, 1)], (1, 0), (1, 1))
+    add([(P, 5), (E, 8), (P, 6), (J, 1)], (0, 2), (1, 2))
+    add([(E, 9), (P, 7), (P, 8), (E, 10), (C, 2)], (2, 0), (2, 1))
+    add([(P, 9)], (2, 2))
+    add([(E, 11), (J, 2)], (0, 3))
+    add([(P, 10), (E, 12)], (1, 3), (2, 3))
+    add([(P, 11), (E, 13), (C, 3)], (3, 0), (3, 1), (3, 2), (3, 3))
+    add([(E, 14), (J, 3)], (0, 4), (1, 4))
+    add([(E, 15)], (2, 4))
+    add([(E, 16)], (3, 4))
+    add([(C, 4)], (4, 0), (4, 1), (4, 2), (4, 3), (4, 4))
+
+    def unit(u, _):
+        for k, (events, _unit) in enumerate(plan):
+            if events:
+
+                @pl.when(u == k)
+                def _():
+                    for call, argument in events:
+                        call(argument)
+
+        r, j = 0, 0
+        for k, (_events, (unit_r, unit_j)) in enumerate(plan):
+            r = r + jnp.where(u == k, unit_r, 0)
+            j = j + jnp.where(u == k, unit_j, 0)
+        pl.when(r < cands - 1)(lambda: whole_unit(r, j))
+        pl.when(r >= cands - 1)(lambda: half_unit(r, j))
         return 0
 
     lax.fori_loop(0, len(plan), unit, 0)
@@ -658,9 +710,10 @@
 ):
     rows, part = cand_inputs.shape
     tps = lax.axis_size("tp")
-    floors, chunks, wide = tps // 2, rows // CLEN, 2 * HEAD
+    cands, wide = rows // CLEN, 2 * HEAD
+    chunks = len(chunk_bounds(rows))
     columns = w_query.shape[1] // wide
-    pieces = 2 + 2 * columns
+    pieces = len(piece_table(columns, w_query.shape[0] // 2))
     prompt_rows = prompt_inputs.shape[0]
     half_freq = ROPE_THETA ** (-np.arange(HEAD // 2, dtype=np.float64) * 2.0 / HEAD)
     freq = jnp.asarray(np.concatenate([half_freq, half_freq]).astype(np.float32).reshape(1, HEAD))
@@ -684,7 +737,7 @@
             pltpu.VMEM((4, HEAD, prompt_rows), jnp.bfloat16),
             pltpu.VMEM((rows, HEAD), jnp.bfloat16),
             pltpu.VMEM((HEAD, rows), jnp.bfloat16),
-            pltpu.VMEM((chunks, 4, prompt_rows, HEAD), jnp.bfloat16),
+            pltpu.VMEM((cands, 4, prompt_rows, HEAD), jnp.bfloat16),
             pltpu.VMEM((2, 4 * prompt_rows + CLEN, CLEN), jnp.float32),
             pltpu.VMEM((columns, rows, wide), jnp.bfloat16),
             dma((4 + columns,)),

time: 180 us -> 172 us (0.956); the launches traced: 178 us -> 172 us
  Pallas kernels: 175 us -> 169 us
    pallas_call x1, Pallas kernels: 175 us -> 169 us  [whole_layer(): pl.pallas_call(layer_kernel, out_shape=jax.ShapeDtypeStruct((rows, column...]
where the time goes in v3:
time: 172 us
  Pallas kernels  169 us (98%)
  local copies, waits for them, and re-layouts  3.08 us (2%)
    pallas_call x1, Pallas kernels, whole_layer(): pl.pallas_call(layer_kernel, out_shape=jax.ShapeDtypeStruct((rows, column...  169 us

profile of v3, /device:TPU:0, one launch (start us, length us, event | category | flops | bytes accessed | tf_op | source)
XLA Modules:
  0.0 172.0 jit_solution(3152672557459059272)
XLA Ops:
  0.0 168.9 %whole_layer.1 = bf16[1024,1024]{1,0:T(8,128)(2,1)} custom-call(bf16[1024,1024]{1,0:T(8,128)(2,1)} %xc_ref.1, bf16[384,8192]{1,0:T(8,128)(2,1)} %xp_ref.1, f32[8,1,1024]{2,1,0:T(1,128)} %bitcast.4, bf16[4096,1024]{1,0:T(8,128)(2,1)} %wq_ref.1, bf16[4096,128]{1,0:T(8,128)(2,1)} %wk_ref.1, bf16[4096,128]{1,0:T(8,128)(2,1)} %wv_ref.1, f32[4,1,256]{2,1,0:T(1,128)} %bitcast.5, ...), custom_call_target="tpu_custom_call" | custom-call | tf_op jit(solution)/shard_map/whole_layer/pallas_call | solution.py:724
  168.9 3.1 %copy.14 = bf16[1024,1024]{1,0:T(8,128)(2,1)} copy(bf16[1024,1024]{1,0:T(8,128)(2,1)} %whole_layer.1) | data formatting | bytes 4194304

commit v4 on v3

--- a/solution.py
+++ b/solution.py
@@ -146,10 +146,10 @@
 
 
 def piece_table(columns, quarter):
-    table = [(0, 0, quarter), (0, 0, quarter)]
+    table = [(0, 0, 0, quarter // 2), (0, 0, quarter // 2, quarter // 2), (0, 1, 0, quarter)]
     for j in range(columns):
         count = 2 if j < columns - 1 else 4
-        table += [(1 + j, n * (quarter // count), quarter // count) for n in range(count)]
+        table += [(1 + j, None, n * (quarter // count), quarter // count) for n in range(count)]
     return table
 
 
@@ -220,16 +220,19 @@
         copy.start()
 
     def piece_place(i, side_y, side_x):
-        j, first, count = table_of_pieces[i]
+        j, side, first, count = table_of_pieces[i]
         where = pl.ds(pl.multiple_of(side_y * half + side_x * quarter + first, count), count)
-        return wts.at[0, where, i * HEAD : (i + 1) * HEAD] if j == 0 else wts.at[j, where, :]
-
-    def direct(i):
-        j, first, count = table_of_pieces[i]
-        where = pl.ds(pl.multiple_of(x * quarter + first, count), count)
-        src = (wk_ref, wv_ref)[i].at[where, :] if j == 0 else wq_ref.at[where, (j - 1) * wide : j * wide]
+        return wts.at[0, where, side * HEAD : (side + 1) * HEAD] if j == 0 else wts.at[j, where, :]
+
+    relayed = pieces - 1
+
+    def direct(n):
+        i, side_x = (n, x) if n < pieces else (pieces - 1, 1 - x)
+        j, side, first, count = table_of_pieces[i]
+        where = pl.ds(pl.multiple_of(side_x * quarter + first, count), count)
+        src = (wk_ref, wv_ref)[side].at[where, :] if j == 0 else wq_ref.at[where, (j - 1) * wide : j * wide]
         return pltpu.make_async_remote_copy(
-            src_ref=src, dst_ref=piece_place(i, y, x), send_sem=wsend.at[i], recv_sem=wrecv.at[i],
+            src_ref=src, dst_ref=piece_place(i, y, side_x), send_sem=wsend.at[n], recv_sem=wrecv.at[n],
             device_id=over, device_id_type=MESH,
         )
 
@@ -241,13 +244,11 @@
         )
 
     def pass_piece(i):
-        if 0 <= i < pieces:
-            direct(i).wait_recv()
-            relay(i).start()
+        direct(i).wait_recv()
+        relay(i).start()
 
     def send_piece(i):
-        if 0 <= i < pieces:
-            direct(i).start()
+        direct(i).start()
 
     def slab(s, r):
         return acts.at[s, pl.ds(*bounds[r]), :]
@@ -303,6 +304,10 @@
 
             pl.when(z == depth)(functools.partial(go, 0, -1, up))
             pl.when(floors - 1 - z == depth)(functools.partial(go, 1, 1, down))
+
+    pl.semaphore_wait(barrier, tps + 2)
+    for i in range(5):
+        send_piece(i)
 
     load_x.wait()
     for r in range(cands):
@@ -315,8 +320,6 @@
             turned = jnp.transpose(lanes[b * HEAD : (b + 1) * HEAD, :])
             stats[tp, :, pl.ds(r * block + b * HEAD, HEAD)] = jnp.sum(turned, axis=0, keepdims=True)
 
-    pl.semaphore_wait(barrier, tps + 2)
-
     def stat_copy(t):
         return pltpu.make_async_remote_copy(
             src_ref=stats.at[tp], dst_ref=stats.at[tp], send_sem=st_send.at[t], recv_sem=st_recv.at[tp],
@@ -332,8 +335,6 @@
 
     for t in range(tps - 1):
         stat_copy(t).start()
-    for i in range(4):
-        send_piece(i)
     for t in range(tps - 1):
         stat_arrival(t).wait_recv()
     total = stats[0]
@@ -392,6 +393,7 @@
         return value * cosine + pltpu.roll(value, HEAD // 2, 1) * sine
 
     pass_piece(0)
+    pass_piece(1)
     link_event(2)
 
     load_p.wait()
@@ -410,9 +412,9 @@
         return 0
 
     lax.fori_loop(0, prompt_rows // slab_rows, norm_prompt, 0)
-    pass_piece(1)
+    pass_piece(2)
     link_event(3)
-    pass_piece(2)
+    pass_piece(3)
     link_event(4)
 
     def await_piece(i):
@@ -424,7 +426,7 @@
 
     load_w[0].wait()
     load_w[1].wait()
-    for i in range(2):
+    for i in range(3):
         await_piece(i)
 
     def prompt_block(b, _):
@@ -453,18 +455,21 @@
     for n in range(3):
         for kind in range(2):
             prompt_copy(n, kind, joined).start()
-    for i in range(4, 7):
+    for i in range(5, 8):
         send_piece(i)
-    pass_piece(3)
+    pass_piece(4)
     link_event(5)
-    for i in range(7, pieces):
+    for i in range(8, pieces + 1):
         send_piece(i)
 
     def await_columns(j):
         load_w[2 + j].wait()
-        for i in range(2, pieces):
-            if table_of_pieces[i][0] == 1 + j:
+        for i in range(pieces):
+            if table_of_pieces[i][0] == 1 + j and i < relayed:
                 await_piece(i)
+        if j == columns - 1:
+            direct(pieces - 1).wait_recv()
+            direct(pieces).wait_recv()
 
     def await_chunk(r):
         for f in range(floors):
@@ -614,16 +619,19 @@
             plan.append((events if n == 0 else [], unit))
 
     E, P, C, J = link_event, pass_piece, await_chunk, await_columns
-    add([(E, 6), (P, 4), (C, 0), (J, 0), (await_prompt, 0)], (0, 0), (0, 1))
-    add([(E, 7), (C, 1)], (1, 0), (1, 1))
-    add([(P, 5), (E, 8), (P, 6), (J, 1)], (0, 2), (1, 2))
-    add([(E, 9), (P, 7), (P, 8), (E, 10), (C, 2)], (2, 0), (2, 1))
-    add([(P, 9)], (2, 2))
-    add([(E, 11), (J, 2)], (0, 3))
-    add([(P, 10), (E, 12)], (1, 3), (2, 3))
-    add([(P, 11), (E, 13), (C, 3)], (3, 0), (3, 1), (3, 2), (3, 3))
-    add([(E, 14), (J, 3)], (0, 4), (1, 4))
-    add([(E, 15)], (2, 4))
+    add([(E, 6), (P, 5), (C, 0), (J, 0), (await_prompt, 0)], (0, 0), (0, 1))
+    add([(E, 7), (C, 1)], (1, 0))
+    add([(P, 6)], (1, 1))
+    add([(E, 8), (P, 7), (J, 1)], (0, 2), (1, 2))
+    add([(E, 9), (P, 8), (P, 9), (E, 10), (C, 2)], (2, 0), (2, 1))
+    add([(P, 10), (E, 11)], (2, 2))
+    add([(P, 11), (J, 2)], (0, 3))
+    add([(E, 12)], (1, 3))
+    add([(E, 13)], (2, 3))
+    add([(C, 3)], (3, 0), (3, 1))
+    add([(E, 14)], (3, 2), (3, 3))
+    add([(J, 3)], (0, 4))
+    add([(E, 15)], (1, 4), (2, 4))
     add([(E, 16)], (3, 4))
     add([(C, 4)], (4, 0), (4, 1), (4, 2), (4, 3), (4, 4))
 
@@ -654,8 +662,9 @@
             prompt_copy(n, kind, joined).wait_send()
     for t in range(tps - 1):
         stat_copy(t).wait_send()
-    for i in range(pieces):
+    for i in range(pieces + 1):
         direct(i).wait_send()
+    for i in range(relayed):
         relay(i).wait_send()
     for r in range(chunks):
         to_sibling(tp, r).wait_send()
@@ -741,8 +750,8 @@
             pltpu.VMEM((2, 4 * prompt_rows + CLEN, CLEN), jnp.float32),
             pltpu.VMEM((columns, rows, wide), jnp.bfloat16),
             dma((4 + columns,)),
-            dma((pieces,)),
-            dma((pieces,)),
+            dma((pieces + 1,)),
+            dma((pieces + 1,)),
             dma((pieces,)),
             dma((pieces,)),
             dma((2, chunks)),

time: 172 us -> 171 us (level)
  Pallas kernels: 169 us -> 167 us
where the time goes in v4:
time: 171 us; the launch traced here: 170 us
  Pallas kernels  167 us (98%)
  local copies, waits for them, and re-layouts  3.08 us (2%)
    pallas_call x1, Pallas kernels, whole_layer(): pl.pallas_call(layer_kernel, out_shape=jax.ShapeDtypeStruct((rows, column...  167 us

profile of v4, /device:TPU:0, one launch (start us, length us, event | category | flops | bytes accessed | tf_op | source)
XLA Modules:
  0.0 170.4 jit_solution(16696740926345873811)
XLA Ops:
  0.0 167.3 %whole_layer.1 = bf16[1024,1024]{1,0:T(8,128)(2,1)} custom-call(bf16[1024,1024]{1,0:T(8,128)(2,1)} %xc_ref.1, bf16[384,8192]{1,0:T(8,128)(2,1)} %xp_ref.1, f32[8,1,1024]{2,1,0:T(1,128)} %bitcast.4, bf16[4096,1024]{1,0:T(8,128)(2,1)} %wq_ref.1, bf16[4096,128]{1,0:T(8,128)(2,1)} %wk_ref.1, bf16[4096,128]{1,0:T(8,128)(2,1)} %wv_ref.1, f32[4,1,256]{2,1,0:T(1,128)} %bitcast.5, ...), custom_call_target="tpu_custom_call" | custom-call | tf_op jit(solution)/shard_map/whole_layer/pallas_call | solution.py:733
  167.3 3.1 %copy.14 = bf16[1024,1024]{1,0:T(8,128)(2,1)} copy(bf16[1024,1024]{1,0:T(8,128)(2,1)} %whole_layer.1) | data formatting | bytes 4194304

commit v5 on v4

--- a/solution.py
+++ b/solution.py
@@ -140,6 +140,9 @@
 MESH = pl.DeviceIdType.MESH
 
 
+EXTRA = 2
+
+
 def chunk_bounds(rows):
     whole = [(first, CLEN) for first in range(0, rows - CLEN, CLEN)]
     return whole + [(rows - CLEN, CLEN // 2), (rows - CLEN // 2, CLEN // 2)]
@@ -224,10 +227,10 @@
         where = pl.ds(pl.multiple_of(side_y * half + side_x * quarter + first, count), count)
         return wts.at[0, where, side * HEAD : (side + 1) * HEAD] if j == 0 else wts.at[j, where, :]
 
-    relayed = pieces - 1
+    relayed = pieces - EXTRA
 
     def direct(n):
-        i, side_x = (n, x) if n < pieces else (pieces - 1, 1 - x)
+        i, side_x = (n, x) if n < pieces else (n - EXTRA, 1 - x)
         j, side, first, count = table_of_pieces[i]
         where = pl.ds(pl.multiple_of(side_x * quarter + first, count), count)
         src = (wk_ref, wv_ref)[side].at[where, :] if j == 0 else wq_ref.at[where, (j - 1) * wide : j * wide]
@@ -459,7 +462,7 @@
         send_piece(i)
     pass_piece(4)
     link_event(5)
-    for i in range(8, pieces + 1):
+    for i in range(8, pieces + EXTRA):
         send_piece(i)
 
     def await_columns(j):
@@ -468,8 +471,8 @@
             if table_of_pieces[i][0] == 1 + j and i < relayed:
                 await_piece(i)
         if j == columns - 1:
-            direct(pieces - 1).wait_recv()
-            direct(pieces).wait_recv()
+            for i in range(relayed, pieces + EXTRA):
+                direct(i).wait_recv()
 
     def await_chunk(r):
         for f in range(floors):
@@ -625,7 +628,7 @@
     add([(E, 8), (P, 7), (J, 1)], (0, 2), (1, 2))
     add([(E, 9), (P, 8), (P, 9), (E, 10), (C, 2)], (2, 0), (2, 1))
     add([(P, 10), (E, 11)], (2, 2))
-    add([(P, 11), (J, 2)], (0, 3))
+    add([(J, 2)], (0, 3))
     add([(E, 12)], (1, 3))
     add([(E, 13)], (2, 3))
     add([(C, 3)], (3, 0), (3, 1))
@@ -662,7 +665,7 @@
             prompt_copy(n, kind, joined).wait_send()
     for t in range(tps - 1):
         stat_copy(t).wait_send()
-    for i in range(pieces + 1):
+    for i in range(pieces + EXTRA):
         direct(i).wait_send()
     for i in range(relayed):
         relay(i).wait_send()
@@ -750,8 +753,8 @@
             pltpu.VMEM((2, 4 * prompt_rows + CLEN, CLEN), jnp.float32),
             pltpu.VMEM((columns, rows, wide), jnp.bfloat16),
             dma((4 + columns,)),
-            dma((pieces + 1,)),
-            dma((pieces + 1,)),
+            dma((pieces + EXTRA,)),
+            dma((pieces + EXTRA,)),
             dma((pieces,)),
             dma((pieces,)),
             dma((2, chunks)),

time: 171 us -> 170 us (level)
  no operation moved by 1% of the time
where the time goes in v5:
time: 170 us
  Pallas kernels  167 us (98%)
  local copies, waits for them, and re-layouts  3.08 us (2%)
    pallas_call x1, Pallas kernels, whole_layer(): pl.pallas_call(layer_kernel, out_shape=jax.ShapeDtypeStruct((rows, column...  167 us

profile of v5, /device:TPU:0, one launch (start us, length us, event | category | flops | bytes accessed | tf_op | source)
XLA Modules:
  0.0 170.0 jit_solution(8412776281101548671)
XLA Ops:
  0.0 167.0 %whole_layer.1 = bf16[1024,1024]{1,0:T(8,128)(2,1)} custom-call(bf16[1024,1024]{1,0:T(8,128)(2,1)} %xc_ref.1, bf16[384,8192]{1,0:T(8,128)(2,1)} %xp_ref.1, f32[8,1,1024]{2,1,0:T(1,128)} %bitcast.4, bf16[4096,1024]{1,0:T(8,128)(2,1)} %wq_ref.1, bf16[4096,128]{1,0:T(8,128)(2,1)} %wk_ref.1, bf16[4096,128]{1,0:T(8,128)(2,1)} %wv_ref.1, f32[4,1,256]{2,1,0:T(1,128)} %bitcast.5, ...), custom_call_target="tpu_custom_call" | custom-call | tf_op jit(solution)/shard_map/whole_layer/pallas_call | solution.py:736
  167.0 3.1 %copy.14 = bf16[1024,1024]{1,0:T(8,128)(2,1)} copy(bf16[1024,1024]{1,0:T(8,128)(2,1)} %whole_layer.1) | data formatting | bytes 4194304
